TPU v7x, 512 devices: a whole 4x4x16 slice. The times are simulated.
512 devices in a mesh: tx: 32 (over y, x, core), ty: 16 (over z).
Axes of the slice: x: 4, y: 4, z: 16, core: 2. Of those that a mesh axis runs over, the one named last changes fastest.
Arguments:
- points: float32 [3, 1048576], P(None, ('tx', 'ty')), may hold values from 0 to 1
- tree_order: int32 [512, 2048], P(('tx', 'ty')), may hold values from 0 to 2047, each once within a row
- samples: float32 [1048576, 128], P(('tx', 'ty')), may hold values from -6 to 6
- near_leaves: int32 [4096, 5], P(('tx', 'ty')), may hold values from 0 to 11, as said below
- near_counts: int32 [4096], P(('tx', 'ty')), may hold values from 0 to 5, as said below
Outputs:
- leaf_bases: float32 [1048576, 128], P(('tx', 'ty'))
- local_bases: float32 [3584, 256, 128], P(('tx', 'ty'))
- upper_bases: float32 [4608, 256, 128], P(('tx', 'ty'))
- root_factor: float32 [128, 128], replicated
Inputs may be any that keep to these rules, and one draw needn't show every extreme that they name: `near_leaves`: for k < near_counts[i], the entry w at [i, k] names the existing leaf (i // 8) * 8 - 2 + w, which is not i; the leaves named in one row are distinct; entries at k >= near_counts[i] are 0. `near_counts`: leaf 0 lists exactly 5 near-field leaves in every draw. `tree_order`: each row is a permutation of the positions of one device's block.
All inputs are finite; a program needn't handle non-finite values.
Results may differ from a plain program's by a relative error of at most 0.0003.
Values sent between devices are 32-bit elements; how exact they have to be, the bound alone decides.
No kernel may reach another device: no remote copies, remote signals or barrier semaphores. Data moves between devices by JAX's collectives and lax.ppermute only.
A program may use at most 64 MiB of HBM per device.

v0:
```python
import jax
import jax.numpy as jnp
from jax import lax
from jax.sharding import PartitionSpec as P

HALO = 2
MAXNB = 5


SPREAD = 50.0


def passed_along(block, axis, distance):
    devices = range(lax.axis_size(axis))
    route = [(i - distance, i) for i in devices if i - distance in devices]
    return lax.ppermute(block, axis, route)


def from_partner(value, axis, stride):
    mask = 2**stride
    pairs = [(source, source ^ mask) for source in range(lax.axis_size(axis))]
    return lax.ppermute(value, axis, pairs)


def orthonormalize(stacked):
    gram_matrix = jnp.einsum(
        "...ir,...is->...rs", stacked, stacked, precision=lax.Precision.HIGHEST
    )
    lower_factor = jnp.linalg.cholesky(gram_matrix)
    basis_rows = jax.scipy.linalg.solve_triangular(
        lower_factor, jnp.swapaxes(stacked, -1, -2), lower=True
    )
    return (jnp.swapaxes(basis_rows, -1, -2), jnp.swapaxes(lower_factor, -1, -2))


def kernel_tile(row_points, column_points, column_samples, weight):
    distance = (row_points[0][:, :, None] - column_points[0][:, None, :]) ** 2
    for coord_index in range(1, 3):
        distance = (
            distance
            + (row_points[coord_index][:, :, None] - column_points[coord_index][:, None, :]) ** 2
        )
    kernel = jnp.exp(-SPREAD * distance) * weight[:, None, None]
    return jnp.einsum("lij,ljr->lir", kernel, column_samples, precision=lax.Precision.HIGHEST)


def join_pair(factor, partner, upper_half):
    stacked = jnp.where(
        upper_half,
        jnp.concatenate([partner, factor], axis=0),
        jnp.concatenate([factor, partner], axis=0),
    )
    return orthonormalize(stacked)


def per_device(points, tree_order, samples, near_leaves, near_counts):
    leaves = near_counts.shape[0]
    rank_width = samples.shape[1]
    leaf_size = samples.shape[0] // leaves
    ordered = jnp.take(points, tree_order[0], axis=1)
    edge_rows = HALO * leaf_size
    whole_before, samples_before = passed_along((ordered, samples), ("tx", "ty"), 1)
    whole_after, samples_after = passed_along((ordered, samples), ("tx", "ty"), -1)
    before_points, before_samples = (whole_before[:, -edge_rows:], samples_before[-edge_rows:])
    after_points, after_samples = (whole_after[:, :edge_rows], samples_after[:edge_rows])
    window_width = leaves + 2 * HALO
    window_points = jnp.concatenate([before_points, ordered, after_points], axis=1).reshape(
        3, window_width, leaf_size
    )
    window_samples = jnp.concatenate([before_samples, samples, after_samples], axis=0).reshape(
        window_width, leaf_size, rank_width
    )
    own_points = ordered.reshape(3, leaves, leaf_size)
    own_samples = samples.reshape(leaves, leaf_size, rank_width)
    sampled = kernel_tile(own_points, own_points, own_samples, jnp.ones((leaves,), jnp.float32))
    for position in range(MAXNB):
        column_leaf = near_leaves[:, position]
        weight = (near_counts > position).astype(jnp.float32)
        sampled = sampled + kernel_tile(
            own_points,
            jnp.take(window_points, column_leaf, axis=1),
            jnp.take(window_samples, column_leaf, axis=0),
            weight,
        )
    leaf_basis, factors = orthonormalize(sampled)
    local_levels = []
    while factors.shape[0] > 1:
        basis, factors = orthonormalize(
            factors.reshape(factors.shape[0] // 2, 2 * rank_width, rank_width)
        )
        local_levels.append(basis)
    local_bases = jnp.concatenate(local_levels, axis=0)
    factor = factors[0]
    collected = []
    for height in range(lax.axis_size("ty").bit_length() - 1):
        partner = from_partner(factor, "ty", height)
        upper_half = lax.axis_index("ty") // 2**height % 2 == 1
        basis, factor = join_pair(factor, partner, upper_half)
        collected.append(basis)
    for height in range(lax.axis_size("tx").bit_length() - 1):
        partner = from_partner(factor, "tx", height)
        upper_half = lax.axis_index("tx") // 2**height % 2 == 1
        basis, factor = join_pair(factor, partner, upper_half)
        collected.append(basis)
    upper_bases = jnp.stack(collected, axis=0)
    return (leaf_basis.reshape(leaves * leaf_size, rank_width), local_bases, upper_bases, factor)


def solution(mesh):
    return jax.shard_map(
        per_device,
        mesh=mesh,
        in_specs=(
            P(None, ("tx", "ty")),
            P(("tx", "ty"), None),
            P(("tx", "ty"), None),
            P(("tx", "ty"), None),
            P(("tx", "ty")),
        ),
        out_specs=(
            P(("tx", "ty"), None),
            P(("tx", "ty"), None, None),
            P(("tx", "ty"), None, None),
            P(),
        ),
        check_vma=False,
    )
```

profile of v0, /device:TPU:24, one launch (start us, length us, event | category | flops | bytes accessed | tf_op | source)
XLA Modules:
  0.0 699.2 jit_solution(3812864351538127251)
XLA Ops:
  0.6 13.2 %collective-permute-start.3 = (f32[2048,128]{1,0:T(8,128)}, f32[2048,128]{1,0:T(8,128)}, u32[]{:S(2)}, u32[]{:S(2)}) collective-permute-start(f32[2048,128]{1,0:T(8,128)} %param.14), channel_id=1, source_target_pairs={{1,0},{2,1},{3,2},{4,3},{5,4},{6,5},{7,6},{8,7},{9,8},{10,9},{11,1... | collective-permute-start | bytes 3145736 | tf_op jit(solution)/shard_map/ppermute | solution.py:16
  18.3 5.5 gather_fusion
  24.5 7.9 %collective-permute-start.1 = (f32[3,2048]{1,0:T(4,128)S(1)}, f32[3,2048]{1,0:T(4,128)S(1)}, u32[]{:S(2)}, u32[]{:S(2)}) collective-permute-start(f32[3,2048]{1,0:T(4,128)S(1)} %copy.127), channel_id=1, source_target_pairs={{1,0},{2,1},{3,2},{4,3},{5,4},{6,5},{7,6},{8,7},{9,8},{10,9},{11,1... | collective-permute-start | bytes 73736 | tf_op jit(solution)/shard_map/ppermute | solution.py:16
  36.5 7.7 %collective-permute-done = f32[3,2048]{1,0:T(4,128)S(1)} collective-permute-done((f32[3,2048]{1,0:T(4,128)S(1)}, f32[3,2048]{1,0:T(4,128)S(1)}, u32[]{:S(2)}, u32[]{:S(2)}) %collective-permute-start) | collective-permute-done | bytes 24608 | tf_op jit(solution)/shard_map/ppermute | solution.py:16
  57.9 4.5 fusion
  62.4 3.7 fusion.12
  66.1 3.7 fusion.24
  69.8 3.7 fusion.36
  73.5 3.7 fusion.48
  77.1 3.5 fusion.83
  82.8 94.3 %custom-call.33 = f32[8,128,128]{2,1,0:T(8,128)S(1)} custom-call(f32[8,128,128]{2,1,0:T(8,128)S(1)} %fusion.149), custom_call_target="Cholesky" | custom-call | tf_op jit(solution)/shard_map/jit(cholesky)/cholesky | solution.py:29
  178.9 46.9 %custom-call.35 = f32[4,128,128]{2,1,0:T(8,128)S(1)} custom-call(f32[4,128,128]{2,1,0:T(8,128)S(1)} %fusion.163), custom_call_target="Cholesky" | custom-call | tf_op jit(solution)/shard_map/jit(cholesky)/cholesky | solution.py:29
  227.7 23.6 %custom-call.37 = f32[2,128,128]{2,1,0:T(8,128)S(1)} custom-call(f32[2,128,128]{2,1,0:T(8,128)S(1)} %fusion.176), custom_call_target="Cholesky" | custom-call | tf_op jit(solution)/shard_map/jit(cholesky)/cholesky | solution.py:29
  252.1 11.7 %custom-call.39 = f32[1,128,128]{2,1,0:T(8,128)S(1)} custom-call(f32[1,128,128]{2,1,0:T(8,128)S(1)} %fusion.187), custom_call_target="Cholesky" | custom-call | tf_op jit(solution)/shard_map/jit(cholesky)/cholesky | solution.py:29
  265.8 78.6 %custom-call.34 = f32[8,1,128,128]{2,3,1,0:T(8,128)S(1)} custom-call(f32[8,1,128,128]{3,2,1,0:T(8,128)S(1)} %get-tuple-element.37), custom_call_target="InvertDiagBlocksLowerTriangular" | custom-call | tf_op jit(solution)/shard_map/jit(_solve_triangular)/vmap()/triangular_solve | solution.py:30
  346.4 9.8 %custom-call.49 = f32[1,128,128]{1,2,0:T(8,128)S(1)} custom-call(f32[1,128,128]{2,1,0:T(8,128)S(1)} %fusion.207), custom_call_target="InvertDiagBlocksLowerTriangular" | custom-call | tf_op jit(solution)/shard_map/jit(_solve_triangular)/triangular_solve/custom-call.8 | solution.py:30
  356.2 19.9 %custom-call.38 = f32[2,1,128,128]{2,3,1,0:T(8,128)S(1)} custom-call(f32[2,1,128,128]{3,2,1,0:T(8,128)S(1)} %get-tuple-element.40), custom_call_target="InvertDiagBlocksLowerTriangular" | custom-call | tf_op jit(solution)/shard_map/jit(_solve_triangular)/vmap()/triangular_solve | solution.py:30
  376.5 40.1 %custom-call.36 = f32[4,1,128,128]{2,3,1,0:T(8,128)S(1)} custom-call(f32[4,1,128,128]{3,2,1,0:T(8,128)} %get-tuple-element.38), custom_call_target="InvertDiagBlocksLowerTriangular" | custom-call | tf_op jit(solution)/shard_map/jit(_solve_triangular)/vmap()/triangular_solve | solution.py:30
  420.4 3.0 collective-permute-done.4
  423.8 11.7 %cholesky.288 = f32[128,128]{1,0:T(8,128)S(1)} custom-call(f32[128,128]{1,0:T(8,128)S(1)} %fusion.205), custom_call_target="Cholesky" | custom-call | tf_op jit(solution)/shard_map/jit(cholesky)/cholesky | solution.py:29
  436.9 9.8 %custom-call.50 = f32[1,128,128]{1,2,0:T(8,128)S(1)} custom-call(f32[1,128,128]{2,1,0:T(8,128)S(1)} %get-tuple-element.59), custom_call_target="InvertDiagBlocksLowerTriangular" | custom-call | tf_op jit(solution)/shard_map/jit(_solve_triangular)/triangular_solve/custom-call.8 | solution.py:30
  449.2 4.7 collective-permute-done.5
  454.3 11.7 %cholesky.299 = f32[128,128]{1,0:T(8,128)S(1)} custom-call(f32[128,128]{1,0:T(8,128)S(1)} %fusion.203), custom_call_target="Cholesky" | custom-call | tf_op jit(solution)/shard_map/jit(cholesky)/cholesky | solution.py:29
  467.3 9.8 %custom-call.51 = f32[1,128,128]{1,2,0:T(8,128)S(1)} custom-call(f32[1,128,128]{2,1,0:T(8,128)S(1)} %get-tuple-element.57), custom_call_target="InvertDiagBlocksLowerTriangular" | custom-call | tf_op jit(solution)/shard_map/jit(_solve_triangular)/triangular_solve/custom-call.8 | solution.py:30
  479.9 8.2 %collective-permute-done.6 = f32[128,128]{0,1:T(8,128)S(1)} collective-permute-done((f32[128,128]{0,1:T(8,128)S(1)}, f32[128,128]{0,1:T(8,128)S(1)}, u32[]{:S(2)}, u32[]{:S(2)}) %collective-permute-start.6) | collective-permute-done | bytes 65568 | tf_op jit(solution)/shard_map/ppermute | solution.py:22
  488.5 11.7 %cholesky.310 = f32[128,128]{1,0:T(8,128)S(1)} custom-call(f32[128,128]{1,0:T(8,128)S(1)} %fusion.201), custom_call_target="Cholesky" | custom-call | tf_op jit(solution)/shard_map/jit(cholesky)/cholesky | solution.py:29
  501.5 9.8 %custom-call.52 = f32[1,128,128]{1,2,0:T(8,128)S(1)} custom-call(f32[1,128,128]{2,1,0:T(8,128)S(1)} %get-tuple-element.55), custom_call_target="InvertDiagBlocksLowerTriangular" | custom-call | tf_op jit(solution)/shard_map/jit(_solve_triangular)/triangular_solve/custom-call.8 | solution.py:30
  511.3 4.3 collective-permute-start.7
  516.0 10.2 %collective-permute-done.7 = f32[128,128]{0,1:T(8,128)S(1)} collective-permute-done((f32[128,128]{0,1:T(8,128)S(1)}, f32[128,128]{0,1:T(8,128)S(1)}, u32[]{:S(2)}, u32[]{:S(2)}) %collective-permute-start.7) | collective-permute-done | bytes 65568 | tf_op jit(solution)/shard_map/ppermute | solution.py:22
  526.6 11.7 %cholesky.321 = f32[128,128]{1,0:T(8,128)S(1)} custom-call(f32[128,128]{1,0:T(8,128)S(1)} %fusion.199), custom_call_target="Cholesky" | custom-call | tf_op jit(solution)/shard_map/jit(cholesky)/cholesky | solution.py:29
  539.7 9.8 %custom-call.53 = f32[1,128,128]{1,2,0:T(8,128)S(1)} custom-call(f32[1,128,128]{2,1,0:T(8,128)S(1)} %get-tuple-element.53), custom_call_target="InvertDiagBlocksLowerTriangular" | custom-call | tf_op jit(solution)/shard_map/jit(_solve_triangular)/triangular_solve/custom-call.8 | solution.py:30
  553.0 11.7 %cholesky.332 = f32[128,128]{1,0:T(8,128)S(1)} custom-call(f32[128,128]{1,0:T(8,128)S(1)} %fusion.197), custom_call_target="Cholesky" | custom-call | tf_op jit(solution)/shard_map/jit(cholesky)/cholesky | solution.py:29
  566.1 9.8 %custom-call.54 = f32[1,128,128]{1,2,0:T(8,128)S(1)} custom-call(f32[1,128,128]{2,1,0:T(8,128)S(1)} %get-tuple-element.51), custom_call_target="InvertDiagBlocksLowerTriangular" | custom-call | tf_op jit(solution)/shard_map/jit(_solve_triangular)/triangular_solve/custom-call.8 | solution.py:30
  575.9 3.2 collective-permute-start.9
  579.5 2.6 collective-permute-done.9
  582.5 11.7 %cholesky.343 = f32[128,128]{1,0:T(8,128)S(1)} custom-call(f32[128,128]{1,0:T(8,128)S(1)} %fusion.195), custom_call_target="Cholesky" | custom-call | tf_op jit(solution)/shard_map/jit(cholesky)/cholesky | solution.py:29
  595.5 9.8 %custom-call.55 = f32[1,128,128]{1,2,0:T(8,128)S(1)} custom-call(f32[1,128,128]{2,1,0:T(8,128)S(1)} %get-tuple-element.49), custom_call_target="InvertDiagBlocksLowerTriangular" | custom-call | tf_op jit(solution)/shard_map/jit(_solve_triangular)/triangular_solve/custom-call.8 | solution.py:30
  605.3 4.8 collective-permute-start.10
  613.4 11.7 %cholesky.354 = f32[128,128]{1,0:T(8,128)S(1)} custom-call(f32[128,128]{1,0:T(8,128)S(1)} %fusion.193), custom_call_target="Cholesky" | custom-call | tf_op jit(solution)/shard_map/jit(cholesky)/cholesky | solution.py:29
  626.4 9.8 %custom-call.56 = f32[1,128,128]{1,2,0:T(8,128)S(1)} custom-call(f32[1,128,128]{2,1,0:T(8,128)S(1)} %get-tuple-element.47), custom_call_target="InvertDiagBlocksLowerTriangular" | custom-call | tf_op jit(solution)/shard_map/jit(_solve_triangular)/triangular_solve/custom-call.8 | solution.py:30
  636.3 3.2 collective-permute-start.11
  639.8 2.7 collective-permute-done.11
  642.8 11.7 %cholesky.365 = f32[128,128]{1,0:T(8,128)S(1)} custom-call(f32[128,128]{1,0:T(8,128)S(1)} %fusion.191), custom_call_target="Cholesky" | custom-call | tf_op jit(solution)/shard_map/jit(cholesky)/cholesky | solution.py:29
  655.9 9.8 %custom-call.57 = f32[1,128,128]{1,2,0:T(8,128)S(1)} custom-call(f32[1,128,128]{2,1,0:T(8,128)S(1)} %get-tuple-element.45), custom_call_target="InvertDiagBlocksLowerTriangular" | custom-call | tf_op jit(solution)/shard_map/jit(_solve_triangular)/triangular_solve/custom-call.8 | solution.py:30
  665.7 3.3 collective-permute-start.12
  669.3 4.0 collective-permute-done.12
  673.8 11.7 %cholesky.376 = f32[128,128]{1,0:T(8,128)S(1)} custom-call(f32[128,128]{1,0:T(8,128)S(1)} %fusion.189), custom_call_target="Cholesky" | custom-call | tf_op jit(solution)/shard_map/jit(cholesky)/cholesky | solution.py:29
  686.8 9.8 %custom-call.58 = f32[1,128,128]{1,2,0:T(8,128)S(1)} custom-call(f32[1,128,128]{2,1,0:T(8,128)S(1)} %get-tuple-element.43), custom_call_target="InvertDiagBlocksLowerTriangular" | custom-call | tf_op jit(solution)/shard_map/jit(_solve_triangular)/triangular_solve/custom-call.8 | solution.py:30
  (188 shorter events, 67.1 us)
Async XLA Ops:
  0.6 47.1 %collective-permute-start.3 = (f32[2048,128]{1,0:T(8,128)}, f32[2048,128]{1,0:T(8,128)}, u32[]{:S(2)}, u32[]{:S(2)}) collective-permute-start(f32[2048,128]{1,0:T(8,128)} %param.14), channel_id=1, source_target_pairs={{1,0},{2,1},{3,2},{4,3},{5,4},{6,5},{7,6},{8,7},{9,8},{10,9},{11,1... | collective-permute-start | bytes 3145736 | tf_op jit(solution)/shard_map/ppermute | solution.py:16
  13.9 34.9 %collective-permute-start.2 = (f32[2048,128]{1,0:T(8,128)}, f32[2048,128]{1,0:T(8,128)}, u32[]{:S(2)}, u32[]{:S(2)}) collective-permute-start(f32[2048,128]{1,0:T(8,128)} %param.14), channel_id=1, source_target_pairs={{0,1},{1,2},{2,3},{3,4},{4,5},{5,6},{6,7},{7,8},{8,9},{9,10},{10,1... | collective-permute-start | bytes 3145736 | tf_op jit(solution)/shard_map/ppermute | solution.py:16
  23.8 10.5 %copy-start.5 = (s32[8,5]{1,0:T(8,128)S(1)}, s32[8,5]{1,0:T(8,128)}, u32[]{:S(2)}) copy-start(s32[8,5]{1,0:T(8,128)} %param.15) | copy-start | bytes 484
  24.5 12.0 %collective-permute-start.1 = (f32[3,2048]{1,0:T(4,128)S(1)}, f32[3,2048]{1,0:T(4,128)S(1)}, u32[]{:S(2)}, u32[]{:S(2)}) collective-permute-start(f32[3,2048]{1,0:T(4,128)S(1)} %copy.127), channel_id=1, source_target_pairs={{1,0},{2,1},{3,2},{4,3},{5,4},{6,5},{7,6},{8,7},{9,8},{10,9},{11,1... | collective-permute-start | bytes 73736 | tf_op jit(solution)/shard_map/ppermute | solution.py:16
  32.4 11.8 %collective-permute-start = (f32[3,2048]{1,0:T(4,128)S(1)}, f32[3,2048]{1,0:T(4,128)S(1)}, u32[]{:S(2)}, u32[]{:S(2)}) collective-permute-start(f32[3,2048]{1,0:T(4,128)S(1)} %copy.127), channel_id=1, source_target_pairs={{0,1},{1,2},{2,3},{3,4},{4,5},{5,6},{6,7},{7,8},{8,9},{9,10},{10,1... | collective-permute-start | bytes 73736 | tf_op jit(solution)/shard_map/ppermute | solution.py:16
  34.6 1.6 copy-start.6
  36.0 13.7 %copy-start = (f32[2048,128]{1,0:T(8,128)S(1)}, f32[2048,128]{1,0:T(8,128)}, u32[]{:S(2)}) copy-start(f32[2048,128]{1,0:T(8,128)} %param.14) | copy-start | bytes 3145732
  57.9 4.5 copy-start.4
  62.4 3.7 copy-start.3
  66.1 3.7 copy-start.2
  69.8 3.7 copy-start.1
  417.2 6.2 collective-permute-start.4
  446.7 7.2 %collective-permute-start.5 = (f32[128,128]{0,1:T(8,128)S(1)}, f32[128,128]{0,1:T(8,128)S(1)}, u32[]{:S(2)}, u32[]{:S(2)}) collective-permute-start(f32[128,128]{0,1:T(8,128)S(1)} %get-tuple-element.58), channel_id=1, source_target_pairs={{0,2},{1,3},{2,0},{3,1},{4,6},{5,7},{6,4},{7,5},{8,10},{9,11},{10,... | collective-permute-start | bytes 196616 | tf_op jit(solution)/shard_map/ppermute | solution.py:22
  477.2 10.9 %collective-permute-start.6 = (f32[128,128]{0,1:T(8,128)S(1)}, f32[128,128]{0,1:T(8,128)S(1)}, u32[]{:S(2)}, u32[]{:S(2)}) collective-permute-start(f32[128,128]{0,1:T(8,128)S(1)} %get-tuple-element.56), channel_id=1, source_target_pairs={{0,4},{1,5},{2,6},{3,7},{4,0},{5,1},{6,2},{7,3},{8,12},{9,13},{10,... | collective-permute-start | bytes 196616 | tf_op jit(solution)/shard_map/ppermute | solution.py:22
  511.3 14.9 %collective-permute-start.7 = (f32[128,128]{0,1:T(8,128)S(1)}, f32[128,128]{0,1:T(8,128)S(1)}, u32[]{:S(2)}, u32[]{:S(2)}) collective-permute-start(f32[128,128]{0,1:T(8,128)S(1)} %get-tuple-element.54), channel_id=1, source_target_pairs={{0,8},{1,9},{2,10},{3,11},{4,12},{5,13},{6,14},{7,15},{8,0},{9,1},... | collective-permute-start | bytes 196616 | tf_op jit(solution)/shard_map/ppermute | solution.py:22
  549.5 3.1 collective-permute-start.8
  575.9 6.2 collective-permute-start.9
  605.3 7.7 %collective-permute-start.10 = (f32[128,128]{0,1:T(8,128)S(1)}, f32[128,128]{0,1:T(8,128)S(1)}, u32[]{:S(2)}, u32[]{:S(2)}) collective-permute-start(f32[128,128]{0,1:T(8,128)S(1)} %get-tuple-element.48), channel_id=1, source_target_pairs={{0,64},{16,80},{32,96},{48,112},{64,0},{80,16},{96,32},{112,48},{1... | collective-permute-start | bytes 196616 | tf_op jit(solution)/shard_map/ppermute | solution.py:22
  636.3 6.2 collective-permute-start.11
  665.7 7.7 %collective-permute-start.12 = (f32[128,128]{0,1:T(8,128)S(1)}, f32[128,128]{0,1:T(8,128)S(1)}, u32[]{:S(2)}, u32[]{:S(2)}) collective-permute-start(f32[128,128]{0,1:T(8,128)S(1)} %get-tuple-element.44), channel_id=1, source_target_pairs={{0,256},{16,272},{32,288},{48,304},{64,320},{80,336},{96,352},{112... | collective-permute-start | bytes 196616 | tf_op jit(solution)/shard_map/ppermute | solution.py:22
where the time goes:
time: 703 us; the launch traced here: 699 us
  other arithmetic  538 us (77%)
  starting transfers between devices  52.4 us (7%)
  waiting for transfers between devices  46.3 us (7%)
  matrix products  35.1 us (5%)
  local copies, waits for them, and re-layouts  25.4 us (4%)
    another operation x40, other arithmetic, orthonormalize(): lower_factor = jnp.linalg.cholesky(gram_matrix)  289 us
    another operation x17, other arithmetic, orthonormalize(): jax.scipy.linalg.solve_triangular(lower_factor, jnp.swapaxes(stacked, -1,...  238 us
    ppermute x9, waiting for transfers between devices, from_partner(): return lax.ppermute(value, axis, pairs)  38.6 us
    ppermute x9, starting transfers between devices, from_partner(): return lax.ppermute(value, axis, pairs)  27.5 us
    ppermute x4, starting transfers between devices, passed_along(): return lax.ppermute(block, axis, route)  24.9 us
    dot_general x6, matrix products, kernel_tile(): jnp.einsum('lij,ljr->lir', kernel, column_samples, precision=lax.Precisio...  22.7 us
  transfers between devices with their start and end apart: 13, of which 10 were waited for; matrix products, arithmetic and copies ran while one was open for 3% of the time, Pallas kernels for 0%

commit v1 on v0

v1 whole, which is shorter than its diff:
```python
import jax
import jax.numpy as jnp
from jax import lax
from jax.experimental import pallas as pl
from jax.experimental.pallas import tpu as pltpu
from jax.sharding import PartitionSpec as P

HALO = 2
SPREAD = 50.0
F32 = jnp.float32
BF16 = jnp.bfloat16
BLK = 8
PARAMS = dict(vmem_limit_bytes=56 << 20)


def passed_along(block, axis, distance):
    devices = range(lax.axis_size(axis))
    route = [(i - distance, i) for i in devices if i - distance in devices]
    return lax.ppermute(block, axis, route)


def from_partner(value, axis, stride):
    mask = 2**stride
    pairs = [(source, source ^ mask) for source in range(lax.axis_size(axis))]
    return lax.ppermute(value, axis, pairs)


def pieces(x):
    a = x.astype(BF16).astype(F32)
    y = x - a
    b = y.astype(BF16).astype(F32)
    return a, b, y - b


def row_of(x, j):
    return jnp.broadcast_to(x[j : j + 1, :], x.shape)


def factor_groups(work, groups):
    lane = lax.broadcasted_iota(jnp.int32, (BLK, 128), 1)
    sub = lax.broadcasted_iota(jnp.int32, (BLK, 128), 0)
    for k in range(128 // BLK):
        r = BLK * k
        for group in groups:
            rows_a = {m: work[m, r : r + BLK, :128] for m in group}
            rows_i = {m: work[m, r : r + BLK, 128:] for m in group}
            diag = None
            for s, m in enumerate(group):
                shift = (BLK * s - r) % 128
                x = pltpu.roll(rows_a[m], shift, 1) if shift else rows_a[m]
                diag = x if s == 0 else jnp.where((lane >= BLK * s) & (lane < BLK * (s + 1)), x, diag)
            cols = [pltpu.roll(diag, 128 - j, 1) if j else diag for j in range(BLK)]
            inv = [jnp.where(sub == j, 1.0, 0.0).astype(F32) for j in range(BLK)]
            scale = jnp.ones((BLK, 128), F32)
            for j in range(BLK):
                rs = lax.rsqrt(row_of(cols[j], j))
                mult = jnp.where(sub > j, cols[j] * (rs * rs), 0.0)
                for q in range(j + 1, BLK):
                    cols[q] = cols[q] - mult * row_of(cols[q], j)
                for q in range(j + 1):
                    inv[q] = inv[q] - mult * row_of(inv[q], j)
                scale = jnp.where(sub == j, rs, scale)
            inv = [e * scale for e in inv]
            for s, m in enumerate(group):
                a = i = None
                for q in range(BLK):
                    x = jnp.broadcast_to(inv[q][:, BLK * s : BLK * s + 1], (BLK, 128))
                    ta = x * row_of(rows_a[m], q)
                    ti = x * row_of(rows_i[m], q)
                    a = ta if a is None else a + ta
                    i = ti if i is None else i + ti
                a = jnp.where(lane >= r + sub, a, 0.0)
                work[m, r : r + BLK, :128] = a
                work[m, r : r + BLK, 128:] = i
                if k < 128 // BLK - 1:
                    p1, p2, p3 = pieces(jnp.concatenate([a, i], axis=1))
                    rhs = jnp.concatenate([p1, p2, p1, p2, p3, p1], axis=0).astype(BF16)
                    lhs = jnp.concatenate([p1, p1, p2, p2, p1, p3], axis=0)[:, :128]
                    lhs = lhs.T[r + BLK :].astype(BF16)
                    update = lax.dot_general(lhs, rhs, (((1,), (0,)), ((), ())), preferred_element_type=F32)
                    work[m, r + BLK :, :] = work[m, r + BLK :, :] - update


def times_transposed(x, y):
    return lax.dot_general(
        x, y, (((1,), (1,)), ((), ())), precision=lax.Precision.HIGHEST, preferred_element_type=F32
    )


def identity():
    i = lax.broadcasted_iota(jnp.int32, (128, 128), 0)
    j = lax.broadcasted_iota(jnp.int32, (128, 128), 1)
    return (i == j).astype(F32)


def sample_kernel(
    near, counts, own_points, before_points, after_points, own, before, after, y_ref, g_ref, points, parts
):
    leaves = counts.shape[0]
    for w in range(leaves + 2 * HALO):
        if w < HALO:
            p, s, at = before_points, before, w
        elif w < leaves + HALO:
            p, s, at = own_points, own, w - HALO
        else:
            p, s, at = after_points, after, w - HALO - leaves
        points[w, 0:3, :] = p[:, at * 256 : at * 256 + 256]
        block = s[at * 256 : at * 256 + 256, :]
        high = block.astype(BF16)
        parts[w, :, :128] = high
        parts[w, :, 128:] = (block - high.astype(F32)).astype(BF16)

    def leaf(i, carry):
        rows = points[HALO + i].T

        def tile(w):
            cols = points[w]
            d = None
            for t in range(3):
                e = (rows[:, t : t + 1] - cols[t : t + 1, :]) ** 2
                d = e if d is None else d + e
            kernel = jnp.exp(-SPREAD * d)
            high = kernel.astype(BF16)
            low = (kernel - high.astype(F32)).astype(BF16)
            both = parts[w]
            out = jnp.dot(high, both, preferred_element_type=F32) + jnp.dot(
                low, both, preferred_element_type=F32
            )
            return out[:, :128] + out[:, 128:]

        y_ref[i] = tile(HALO + i)

        def near_one(k, c):
            y_ref[i] = y_ref[i] + tile(near[i, k])
            return c

        lax.fori_loop(0, counts[i], near_one, 0)
        y = y_ref[i]
        g_ref[i] = lax.dot_general(
            y, y, (((0,), (0,)), ((), ())), precision=lax.Precision.HIGHEST, preferred_element_type=F32
        )
        return carry

    lax.fori_loop(0, leaves, leaf, 0)
    at = 0
    n = leaves
    while n > 1:
        for c in range(n // 2):
            g_ref[at + n + c] = g_ref[at + 2 * c] + g_ref[at + 2 * c + 1]
        at += n
        n //= 2


def local_kernel(g_ref, y_ref, leaf_ref, base_ref, root_ref, work):
    total = g_ref.shape[0]
    leaves = (total + 1) // 2
    eye = identity()
    for m in range(total):
        work[m, :, :128] = g_ref[m]
        work[m, :, 128:] = eye
    factor_groups(work, [list(range(total))])
    for m in range(leaves):
        leaf_ref[m * 256 : m * 256 + 256, :] = times_transposed(y_ref[m], work[m, :, 128:])
    for n in range(leaves, total):
        c = 2 * (n - leaves)
        for half in range(2):
            base_ref[n - leaves, half * 128 : half * 128 + 128, :] = times_transposed(
                work[c + half, :, :128], work[n, :, 128:]
            )
    root_ref[...] = work[total - 1, :, :128]


def upper_kernel(flags, root_in, own_ref, partner_ref, base_ref, root_ref, work):
    levels = own_ref.shape[0]
    eye = identity()
    for m in range(levels):
        work[m, :, :128] = own_ref[m]
        work[m, :, 128:] = eye
        work[levels + m, :, :128] = partner_ref[m]
        work[levels + m, :, 128:] = eye
    factor_groups(work, [list(range(levels)), list(range(levels, 2 * levels))])
    for h in range(levels):
        mine = root_in[...] if h == 0 else work[h - 1, :, :128]
        other = work[levels + h, :, :128]
        inverse = work[h, :, 128:]
        a = times_transposed(mine, inverse)
        b = times_transposed(other, inverse)
        upper = flags[h] == 1
        base_ref[h, :128, :] = jnp.where(upper, b, a)
        base_ref[h, 128:, :] = jnp.where(upper, a, b)
    root_ref[...] = work[levels - 1, :, :128]


def call(kernel, outs, scratch, prefetch, args):
    vmem = pl.BlockSpec(memory_space=pltpu.VMEM)
    smem = pl.BlockSpec(memory_space=pltpu.SMEM)
    return pl.pallas_call(
        kernel,
        out_shape=tuple(jax.ShapeDtypeStruct(s, F32) for s in outs),
        in_specs=[smem] * prefetch + [vmem] * (len(args) - prefetch),
        out_specs=tuple([vmem] * len(outs)),
        scratch_shapes=scratch,
        compiler_params=pltpu.CompilerParams(**PARAMS),
    )(*args)


def per_device(points, tree_order, samples, near_leaves, near_counts):
    leaves = near_counts.shape[0]
    both = ("tx", "ty")
    edge = HALO * 256
    before = passed_along(samples[-edge:], both, 1)
    after = passed_along(samples[:edge], both, -1)
    ordered = jnp.take(points, tree_order[0], axis=1)
    before_points = passed_along(ordered[:, -edge:], both, 1)
    after_points = passed_along(ordered[:, :edge], both, -1)
    window = leaves + 2 * HALO
    nodes = 2 * leaves - 1
    sampled, grams = call(
        sample_kernel,
        [(leaves, 256, 128), (nodes, 128, 128)],
        [pltpu.VMEM((window, 8, 256), F32), pltpu.VMEM((window, 256, 256), BF16)],
        2,
        (near_leaves, near_counts, ordered, before_points, after_points, samples, before, after),
    )
    gram = grams[nodes - 1]
    owns, partners, flags = [], [], []
    for axis in ("ty", "tx"):
        for height in range(lax.axis_size(axis).bit_length() - 1):
            partner = from_partner(gram, axis, height)
            gram = gram + partner
            owns.append(gram)
            partners.append(partner)
            flags.append(lax.axis_index(axis) // 2**height % 2)
    leaf_bases, local_bases, local_root = call(
        local_kernel,
        [(leaves * 256, 128), (leaves - 1, 256, 128), (128, 128)],
        [pltpu.VMEM((nodes, 128, 256), F32)],
        0,
        (grams, sampled),
    )
    levels = len(owns)
    upper_bases, root = call(
        upper_kernel,
        [(levels, 256, 128), (128, 128)],
        [pltpu.VMEM((2 * levels, 128, 256), F32)],
        1,
        (jnp.stack(flags), local_root, jnp.stack(owns), jnp.stack(partners)),
    )
    return leaf_bases, local_bases, upper_bases, root


def solution(mesh):
    return jax.shard_map(
        per_device,
        mesh=mesh,
        in_specs=(
            P(None, ("tx", "ty")),
            P(("tx", "ty"), None),
            P(("tx", "ty"), None),
            P(("tx", "ty"), None),
            P(("tx", "ty")),
        ),
        out_specs=(
            P(("tx", "ty"), None),
            P(("tx", "ty"), None, None),
            P(("tx", "ty"), None, None),
            P(),
        ),
        check_vma=False,
    )
```

time: 703 us -> 174 us (0.25)
  other arithmetic: 538 us -> 2.41 us
  Pallas kernels: 0 us -> 52.8 us
  matrix products: 35.1 us -> 0 us
  local copies, waits for them, and re-layouts: 25.4 us -> 11.9 us
  waiting for transfers between devices: 46.3 us -> 55.2 us
    another operation x57 -> x1, other arithmetic: 527 us -> 0.01 us  [per_device(): jnp.stack(partners)]
    pallas_call x0 -> x3, Pallas kernels: none -> 52.8 us  [call(): pl.pallas_call(kernel, out_shape=tuple((jax.ShapeDtypeStruct(s, F32) for...]
    dot_general x19 -> x0, matrix products: 29 us -> none  [the longest x6 22.7 us: kernel_tile(): jnp.einsum('lij,ljr->lir', kernel, column_samples, precision=lax.Precisio...]
    gather x10 -> x0, local copies, waits for them, and re-layouts: 10.9 us -> none  [the longest x5 8.01 us: per_device(): jnp.take(window_samples, column_leaf, axis=0)]
    ppermute x9, waiting for transfers between devices: 38.6 us -> 47.9 us  [from_partner(): return lax.ppermute(value, axis, pairs)]
  transfers between devices with their start and end apart: 13 -> 13, of which waited for: 10 -> 9; matrix products, arithmetic and copies ran while one was open for 3% -> 5% of each run, Pallas kernels for 0% -> 11%
where the time goes in v1:
time: 174 us; the launch traced here: 173 us
  waiting for transfers between devices  55.2 us (32%)
  Pallas kernels  52.8 us (30%)
  starting transfers between devices  49.3 us (28%)
  local copies, waits for them, and re-layouts  11.9 us (7%)
  other arithmetic  2.41 us (1%)
    pallas_call x3, Pallas kernels, call(): pl.pallas_call(kernel, out_shape=tuple((jax.ShapeDtypeStruct(s, F32) for...  52.8 us
    ppermute x9, waiting for transfers between devices, from_partner(): return lax.ppermute(value, axis, pairs)  47.9 us
    ppermute x4, starting transfers between devices, passed_along(): return lax.ppermute(block, axis, route)  24.9 us
    ppermute x9, starting transfers between devices, from_partner(): return lax.ppermute(value, axis, pairs)  24.4 us
    ppermute x4, waiting for transfers between devices, passed_along(): return lax.ppermute(block, axis, route)  7.25 us
    gather x2, local copies, waits for them, and re-layouts, per_device(): ordered = jnp.take(points, tree_order[0], axis=1)  5.79 us
    unnamed x15, local copies, waits for them, and re-layouts  3.52 us
  transfers between devices with their start and end apart: 13, of which 9 were waited for; matrix products, arithmetic and copies ran while one was open for 5% of the time, Pallas kernels for 11%

profile of v1, /device:TPU:24, one launch (start us, length us, event | category | flops | bytes accessed | tf_op | source)
XLA Modules:
  0.0 172.6 jit_solution(3930198205627029088)
XLA Ops:
  0.6 1.1 fusion.2
  1.7 13.2 %collective-permute-start.3 = (f32[512,128]{1,0:T(8,128)S(1)}, f32[512,128]{1,0:T(8,128)S(1)}, u32[]{:S(2)}, u32[]{:S(2)}) collective-permute-start(f32[512,128]{1,0:T(8,128)S(1)} %get-tuple-element.34), channel_id=1, source_target_pairs={{1,0},{2,1},{3,2},{4,3},{5,4},{6,5},{7,6},{8,7},{9,8},{10,9},{11,1... | collective-permute-start | bytes 786440 | tf_op jit(solution)/shard_map/ppermute | solution.py:19
  14.9 1.9 %collective-permute-start.2 = (f32[512,128]{1,0:T(8,128)S(1)}, f32[512,128]{1,0:T(8,128)S(1)}, u32[]{:S(2)}, u32[]{:S(2)}) collective-permute-start(f32[512,128]{1,0:T(8,128)S(1)} %get-tuple-element.35), channel_id=1, source_target_pairs={{0,1},{1,2},{2,3},{3,4},{4,5},{5,6},{6,7},{7,8},{8,9},{9,10},{10,1... | collective-permute-start | bytes 786440 | tf_op jit(solution)/shard_map/ppermute | solution.py:19
  16.9 0.7 compare_select_fusion
  17.6 0.7 compare_and_fusion
  18.3 1.1 copy.11
  19.4 5.5 %gather_fusion = f32[2048,3]{1,0:T(8,128)S(1)} fusion(f32[3,2048]{0,1:T(8,128)S(1)} %copy.11, s32[2048]{0:T(1024)S(1)} %broadcast_clamp_fusion), kind=kCustom, calls=%fused_computation | custom fusion | bytes 57344 | tf_op jit(solution)/shard_map/jit(_take)/gather | solution.py:213
  24.9 0.3 copy.12
  25.2 0.0 copy-start.4
  25.3 7.9 %collective-permute-start.1 = (f32[3,512]{1,0:T(4,128)S(1)}, f32[3,512]{1,0:T(4,128)S(1)}, u32[]{:S(2)}, u32[]{:S(2)}) collective-permute-start(f32[3,512]{1,0:T(4,128)S(1)} %get-tuple-element.46), channel_id=1, source_target_pairs={{1,0},{2,1},{3,2},{4,3},{5,4},{6,5},{7,6},{8,7},{9,8},{10,9},{11,1... | collective-permute-start | bytes 18440 | tf_op jit(solution)/shard_map/ppermute | solution.py:19
  33.1 1.9 %collective-permute-start = (f32[3,512]{1,0:T(4,128)S(1)}, f32[3,512]{1,0:T(4,128)S(1)}, u32[]{:S(2)}, u32[]{:S(2)}) collective-permute-start(f32[3,512]{1,0:T(4,128)S(1)} %get-tuple-element.47), channel_id=1, source_target_pairs={{0,1},{1,2},{2,3},{3,4},{4,5},{5,6},{6,7},{7,8},{8,9},{9,10},{10,1... | collective-permute-start | bytes 18440 | tf_op jit(solution)/shard_map/ppermute | solution.py:19
  35.1 0.0 collective-permute-done.1.after_points
  35.1 0.0 copy-start.5
  35.1 7.2 %collective-permute-done.before_points = f32[3,512]{1,0:T(4,128)S(1)} collective-permute-done((f32[3,512]{1,0:T(4,128)S(1)}, f32[3,512]{1,0:T(4,128)S(1)}, u32[]{:S(2)}, u32[]{:S(2)}) %collective-permute-start) | collective-permute-done | bytes 6176 | tf_op jit(solution)/shard_map/ppermute | solution.py:19
  42.3 0.0 collective-permute-done.3.after
  42.3 0.0 collective-permute-done.2.before
  42.3 0.0 copy-done.4
  42.4 0.6 copy-done.6
  42.9 0.1 copy-done.2
  43.0 0.7 copy-done.3
  43.7 12.3 %shard_map.84 = (f32[8,256,128]{2,1,0:T(8,128)}, f32[15,128,128]{2,1,0:T(8,128)}) custom-call(s32[8,5]{1,0:T(8,128)} %near.1, s32[8]{0:T(128)} %counts.1, f32[3,2048]{1,0:T(4,128)} %copy-done.4, f32[3,512]{1,0:T(4,128)} %copy-done.6, f32[3,512]{1,0:T(4,128)} %copy-done.5, f32[2048,128]{1,0:T(8,128)} %own.1, f32[512,128]{1,0:T(8,128)} %copy-done.3, ...), custom_call_target="tpu_custom_call" | custom-call | tf_op jit(solution)/shard_map/pallas_call | solution.py:197
  56.0 0.8 slice_bitcast_fusion
  56.9 1.9 %collective-permute-start.4 = (f32[128,128]{1,0:T(8,128)S(1)}, f32[128,128]{1,0:T(8,128)S(1)}, u32[]{:S(2)}, u32[]{:S(2)}) collective-permute-start(f32[128,128]{1,0:T(8,128)S(1)} %slice_bitcast_fusion), channel_id=1, source_target_pairs={{0,1},{1,0},{2,3},{3,2},{4,5},{5,4},{6,7},{7,6},{8,9},{9,8},{10,11... | collective-permute-start | bytes 196616 | tf_op jit(solution)/shard_map/ppermute | solution.py:25
  58.8 4.2 %collective-permute-done.4 = f32[128,128]{1,0:T(8,128)S(1)} collective-permute-done((f32[128,128]{1,0:T(8,128)S(1)}, f32[128,128]{1,0:T(8,128)S(1)}, u32[]{:S(2)}, u32[]{:S(2)}) %collective-permute-start.4) | collective-permute-done | bytes 65568 | tf_op jit(solution)/shard_map/ppermute | solution.py:25
  63.0 0.9 bitcast_dynamic-update-slice_fusion.17
  63.9 1.9 %collective-permute-start.5 = (f32[128,128]{1,0:T(8,128)S(1)}, f32[128,128]{1,0:T(8,128)S(1)}, u32[]{:S(2)}, u32[]{:S(2)}) collective-permute-start(f32[128,128]{1,0:T(8,128)S(1)} %get-tuple-element.33), channel_id=1, source_target_pairs={{0,2},{1,3},{2,0},{3,1},{4,6},{5,7},{6,4},{7,5},{8,10},{9,11},{10,... | collective-permute-start | bytes 196616 | tf_op jit(solution)/shard_map/ppermute | solution.py:25
  65.8 6.7 %collective-permute-done.5 = f32[128,128]{1,0:T(8,128)S(1)} collective-permute-done((f32[128,128]{1,0:T(8,128)S(1)}, f32[128,128]{1,0:T(8,128)S(1)}, u32[]{:S(2)}, u32[]{:S(2)}) %collective-permute-start.5) | collective-permute-done | bytes 65568 | tf_op jit(solution)/shard_map/ppermute | solution.py:25
  72.5 1.9 %collective-permute-start.6 = (f32[128,128]{1,0:T(8,128)S(1)}, f32[128,128]{1,0:T(8,128)S(1)}, u32[]{:S(2)}, u32[]{:S(2)}) collective-permute-start(f32[128,128]{1,0:T(8,128)S(1)} %get-tuple-element.31), channel_id=1, source_target_pairs={{0,4},{1,5},{2,6},{3,7},{4,0},{5,1},{6,2},{7,3},{8,12},{9,13},{10,... | collective-permute-start | bytes 196616 | tf_op jit(solution)/shard_map/ppermute | solution.py:25
  74.4 10.7 %collective-permute-done.6 = f32[128,128]{1,0:T(8,128)S(1)} collective-permute-done((f32[128,128]{1,0:T(8,128)S(1)}, f32[128,128]{1,0:T(8,128)S(1)}, u32[]{:S(2)}, u32[]{:S(2)}) %collective-permute-start.6) | collective-permute-done | bytes 65568 | tf_op jit(solution)/shard_map/ppermute | solution.py:25
  85.1 1.9 %collective-permute-start.7 = (f32[128,128]{1,0:T(8,128)S(1)}, f32[128,128]{1,0:T(8,128)S(1)}, u32[]{:S(2)}, u32[]{:S(2)}) collective-permute-start(f32[128,128]{1,0:T(8,128)S(1)} %get-tuple-element.29), channel_id=1, source_target_pairs={{0,8},{1,9},{2,10},{3,11},{4,12},{5,13},{6,14},{7,15},{8,0},{9,1},... | collective-permute-start | bytes 196616 | tf_op jit(solution)/shard_map/ppermute | solution.py:25
  87.0 12.9 %collective-permute-done.7 = f32[128,128]{1,0:T(8,128)S(1)} collective-permute-done((f32[128,128]{1,0:T(8,128)S(1)}, f32[128,128]{1,0:T(8,128)S(1)}, u32[]{:S(2)}, u32[]{:S(2)}) %collective-permute-start.7) | collective-permute-done | bytes 65568 | tf_op jit(solution)/shard_map/ppermute | solution.py:25
  100.0 1.9 %collective-permute-start.8 = (f32[128,128]{1,0:T(8,128)S(1)}, f32[128,128]{1,0:T(8,128)S(1)}, u32[]{:S(2)}, u32[]{:S(2)}) collective-permute-start(f32[128,128]{1,0:T(8,128)S(1)} %get-tuple-element.27), channel_id=1, source_target_pairs={{0,16},{16,0},{32,48},{48,32},{64,80},{80,64},{96,112},{112,96},{1... | collective-permute-start | bytes 196616 | tf_op jit(solution)/shard_map/ppermute | solution.py:25
  101.9 1.2 collective-permute-done.8
  103.1 1.9 %collective-permute-start.9 = (f32[128,128]{1,0:T(8,128)S(1)}, f32[128,128]{1,0:T(8,128)S(1)}, u32[]{:S(2)}, u32[]{:S(2)}) collective-permute-start(f32[128,128]{1,0:T(8,128)S(1)} %get-tuple-element.25), channel_id=1, source_target_pairs={{0,32},{16,48},{32,0},{48,16},{64,96},{80,112},{96,64},{112,80},{1... | collective-permute-start | bytes 196616 | tf_op jit(solution)/shard_map/ppermute | solution.py:25
  105.1 4.2 %collective-permute-done.9 = f32[128,128]{1,0:T(8,128)S(1)} collective-permute-done((f32[128,128]{1,0:T(8,128)S(1)}, f32[128,128]{1,0:T(8,128)S(1)}, u32[]{:S(2)}, u32[]{:S(2)}) %collective-permute-start.9) | collective-permute-done | bytes 65568 | tf_op jit(solution)/shard_map/ppermute | solution.py:25
  109.3 1.9 %collective-permute-start.10 = (f32[128,128]{1,0:T(8,128)S(1)}, f32[128,128]{1,0:T(8,128)S(1)}, u32[]{:S(2)}, u32[]{:S(2)}) collective-permute-start(f32[128,128]{1,0:T(8,128)S(1)} %get-tuple-element.23), channel_id=1, source_target_pairs={{0,64},{16,80},{32,96},{48,112},{64,0},{80,16},{96,32},{112,48},{1... | collective-permute-start | bytes 196616 | tf_op jit(solution)/shard_map/ppermute | solution.py:25
  111.3 5.7 %collective-permute-done.10 = f32[128,128]{1,0:T(8,128)S(1)} collective-permute-done((f32[128,128]{1,0:T(8,128)S(1)}, f32[128,128]{1,0:T(8,128)S(1)}, u32[]{:S(2)}, u32[]{:S(2)}) %collective-permute-start.10) | collective-permute-done | bytes 65568 | tf_op jit(solution)/shard_map/ppermute | solution.py:25
  117.0 6.2 %collective-permute-start.11 = (f32[128,128]{1,0:T(8,128)S(1)}, f32[128,128]{1,0:T(8,128)S(1)}, u32[]{:S(2)}, u32[]{:S(2)}) collective-permute-start(f32[128,128]{1,0:T(8,128)S(1)} %get-tuple-element.21), channel_id=1, source_target_pairs={{0,128},{16,144},{32,160},{48,176},{64,192},{80,208},{96,224},{112... | collective-permute-start | bytes 196616 | tf_op jit(solution)/shard_map/ppermute | solution.py:25
  123.2 2.2 %collective-permute-done.11 = f32[128,128]{1,0:T(8,128)S(1)} collective-permute-done((f32[128,128]{1,0:T(8,128)S(1)}, f32[128,128]{1,0:T(8,128)S(1)}, u32[]{:S(2)}, u32[]{:S(2)}) %collective-permute-start.11) | collective-permute-done | bytes 65568 | tf_op jit(solution)/shard_map/ppermute | solution.py:25
  125.5 4.7 %collective-permute-start.12 = (f32[128,128]{1,0:T(8,128)S(1)}, f32[128,128]{1,0:T(8,128)S(1)}, u32[]{:S(2)}, u32[]{:S(2)}) collective-permute-start(f32[128,128]{1,0:T(8,128)S(1)} %get-tuple-element.19), channel_id=1, source_target_pairs={{0,256},{16,272},{32,288},{48,304},{64,320},{80,336},{96,352},{112... | collective-permute-start | bytes 196616 | tf_op jit(solution)/shard_map/ppermute | solution.py:25
  130.4 0.7 stack.99.flags
  131.1 18.6 %shard_map.85 = (f32[2048,128]{1,0:T(8,128)}, f32[7,256,128]{2,1,0:T(8,128)}, f32[128,128]{1,0:T(8,128)}) custom-call(f32[15,128,128]{2,1,0:T(8,128)} %get-tuple-element.11.g_ref, f32[8,256,128]{2,1,0:T(8,128)} %get-tuple-element.12.y_ref), custom_call_target="tpu_custom_call" | custom-call | tf_op jit(solution)/shard_map/pallas_call | solution.py:197
  149.6 0.0 collective-permute-done.12
  149.7 0.0 copy-start
  149.7 0.0 copy-start.1
  149.7 0.8 copy-done
  150.5 0.2 copy-done.1
  150.7 22.0 %shard_map.86 = (f32[9,256,128]{2,1,0:T(8,128)}, f32[128,128]{1,0:T(8,128)}) custom-call(s32[9]{0:T(128)} %stack.99.flags, f32[128,128]{1,0:T(8,128)} %get-tuple-element.15.root_in, f32[9,128,128]{2,1,0:T(8,128)} %copy-done, f32[9,128,128]{2,1,0:T(8,128)} %copy-done.1), custom_call_target="tpu_custom_call" | custom-call | tf_op jit(solution)/shard_map/pallas_call | solution.py:197
  (15 shorter events, 0.2 us)
Async XLA Ops:
  1.7 40.6 %collective-permute-start.3 = (f32[512,128]{1,0:T(8,128)S(1)}, f32[512,128]{1,0:T(8,128)S(1)}, u32[]{:S(2)}, u32[]{:S(2)}) collective-permute-start(f32[512,128]{1,0:T(8,128)S(1)} %get-tuple-element.34), channel_id=1, source_target_pairs={{1,0},{2,1},{3,2},{4,3},{5,4},{6,5},{7,6},{8,7},{9,8},{10,9},{11,1... | collective-permute-start | bytes 786440 | tf_op jit(solution)/shard_map/ppermute | solution.py:19
  14.9 27.4 %collective-permute-start.2 = (f32[512,128]{1,0:T(8,128)S(1)}, f32[512,128]{1,0:T(8,128)S(1)}, u32[]{:S(2)}, u32[]{:S(2)}) collective-permute-start(f32[512,128]{1,0:T(8,128)S(1)} %get-tuple-element.35), channel_id=1, source_target_pairs={{0,1},{1,2},{2,3},{3,4},{4,5},{5,6},{6,7},{7,8},{8,9},{9,10},{10,1... | collective-permute-start | bytes 786440 | tf_op jit(solution)/shard_map/ppermute | solution.py:19
  25.2 17.1 %copy-start.4 = (f32[3,2048]{1,0:T(4,128)}, f32[3,2048]{1,0:T(4,128)S(1)}, u32[]{:S(2)}) copy-start(f32[3,2048]{1,0:T(4,128)S(1)} %select_bitcast_fusion.own_points) | copy-start | bytes 73732
  25.3 9.8 %collective-permute-start.1 = (f32[3,512]{1,0:T(4,128)S(1)}, f32[3,512]{1,0:T(4,128)S(1)}, u32[]{:S(2)}, u32[]{:S(2)}) collective-permute-start(f32[3,512]{1,0:T(4,128)S(1)} %get-tuple-element.46), channel_id=1, source_target_pairs={{1,0},{2,1},{3,2},{4,3},{5,4},{6,5},{7,6},{8,7},{9,8},{10,9},{11,1... | collective-permute-start | bytes 18440 | tf_op jit(solution)/shard_map/ppermute | solution.py:19
  33.1 9.2 %collective-permute-start = (f32[3,512]{1,0:T(4,128)S(1)}, f32[3,512]{1,0:T(4,128)S(1)}, u32[]{:S(2)}, u32[]{:S(2)}) collective-permute-start(f32[3,512]{1,0:T(4,128)S(1)} %get-tuple-element.47), channel_id=1, source_target_pairs={{0,1},{1,2},{2,3},{3,4},{4,5},{5,6},{6,7},{7,8},{8,9},{9,10},{10,1... | collective-permute-start | bytes 18440 | tf_op jit(solution)/shard_map/ppermute | solution.py:19
  35.1 7.3 %copy-start.5 = (f32[3,512]{1,0:T(4,128)}, f32[3,512]{1,0:T(4,128)S(1)}, u32[]{:S(2)}) copy-start(f32[3,512]{1,0:T(4,128)S(1)} %collective-permute-done.1.after_points) | copy-start | bytes 18436
  42.3 0.6 copy-start.6
  42.3 0.7 copy-start.2
  43.0 0.7 copy-start.3
  56.9 6.1 %collective-permute-start.4 = (f32[128,128]{1,0:T(8,128)S(1)}, f32[128,128]{1,0:T(8,128)S(1)}, u32[]{:S(2)}, u32[]{:S(2)}) collective-permute-start(f32[128,128]{1,0:T(8,128)S(1)} %slice_bitcast_fusion), channel_id=1, source_target_pairs={{0,1},{1,0},{2,3},{3,2},{4,5},{5,4},{6,7},{7,6},{8,9},{9,8},{10,11... | collective-permute-start | bytes 196616 | tf_op jit(solution)/shard_map/ppermute | solution.py:25
  63.9 8.6 %collective-permute-start.5 = (f32[128,128]{1,0:T(8,128)S(1)}, f32[128,128]{1,0:T(8,128)S(1)}, u32[]{:S(2)}, u32[]{:S(2)}) collective-permute-start(f32[128,128]{1,0:T(8,128)S(1)} %get-tuple-element.33), channel_id=1, source_target_pairs={{0,2},{1,3},{2,0},{3,1},{4,6},{5,7},{6,4},{7,5},{8,10},{9,11},{10,... | collective-permute-start | bytes 196616 | tf_op jit(solution)/shard_map/ppermute | solution.py:25
  72.5 12.6 %collective-permute-start.6 = (f32[128,128]{1,0:T(8,128)S(1)}, f32[128,128]{1,0:T(8,128)S(1)}, u32[]{:S(2)}, u32[]{:S(2)}) collective-permute-start(f32[128,128]{1,0:T(8,128)S(1)} %get-tuple-element.31), channel_id=1, source_target_pairs={{0,4},{1,5},{2,6},{3,7},{4,0},{5,1},{6,2},{7,3},{8,12},{9,13},{10,... | collective-permute-start | bytes 196616 | tf_op jit(solution)/shard_map/ppermute | solution.py:25
  85.1 14.9 %collective-permute-start.7 = (f32[128,128]{1,0:T(8,128)S(1)}, f32[128,128]{1,0:T(8,128)S(1)}, u32[]{:S(2)}, u32[]{:S(2)}) collective-permute-start(f32[128,128]{1,0:T(8,128)S(1)} %get-tuple-element.29), channel_id=1, source_target_pairs={{0,8},{1,9},{2,10},{3,11},{4,12},{5,13},{6,14},{7,15},{8,0},{9,1},... | collective-permute-start | bytes 196616 | tf_op jit(solution)/shard_map/ppermute | solution.py:25
  100.0 3.1 %collective-permute-start.8 = (f32[128,128]{1,0:T(8,128)S(1)}, f32[128,128]{1,0:T(8,128)S(1)}, u32[]{:S(2)}, u32[]{:S(2)}) collective-permute-start(f32[128,128]{1,0:T(8,128)S(1)} %get-tuple-element.27), channel_id=1, source_target_pairs={{0,16},{16,0},{32,48},{48,32},{64,80},{80,64},{96,112},{112,96},{1... | collective-permute-start | bytes 196616 | tf_op jit(solution)/shard_map/ppermute | solution.py:25
  103.1 6.2 %collective-permute-start.9 = (f32[128,128]{1,0:T(8,128)S(1)}, f32[128,128]{1,0:T(8,128)S(1)}, u32[]{:S(2)}, u32[]{:S(2)}) collective-permute-start(f32[128,128]{1,0:T(8,128)S(1)} %get-tuple-element.25), channel_id=1, source_target_pairs={{0,32},{16,48},{32,0},{48,16},{64,96},{80,112},{96,64},{112,80},{1... | collective-permute-start | bytes 196616 | tf_op jit(solution)/shard_map/ppermute | solution.py:25
  109.3 7.7 %collective-permute-start.10 = (f32[128,128]{1,0:T(8,128)S(1)}, f32[128,128]{1,0:T(8,128)S(1)}, u32[]{:S(2)}, u32[]{:S(2)}) collective-permute-start(f32[128,128]{1,0:T(8,128)S(1)} %get-tuple-element.23), channel_id=1, source_target_pairs={{0,64},{16,80},{32,96},{48,112},{64,0},{80,16},{96,32},{112,48},{1... | collective-permute-start | bytes 196616 | tf_op jit(solution)/shard_map/ppermute | solution.py:25
  117.0 8.5 %collective-permute-start.11 = (f32[128,128]{1,0:T(8,128)S(1)}, f32[128,128]{1,0:T(8,128)S(1)}, u32[]{:S(2)}, u32[]{:S(2)}) collective-permute-start(f32[128,128]{1,0:T(8,128)S(1)} %get-tuple-element.21), channel_id=1, source_target_pairs={{0,128},{16,144},{32,160},{48,176},{64,192},{80,208},{96,224},{112... | collective-permute-start | bytes 196616 | tf_op jit(solution)/shard_map/ppermute | solution.py:25
  125.5 24.2 %collective-permute-start.12 = (f32[128,128]{1,0:T(8,128)S(1)}, f32[128,128]{1,0:T(8,128)S(1)}, u32[]{:S(2)}, u32[]{:S(2)}) collective-permute-start(f32[128,128]{1,0:T(8,128)S(1)} %get-tuple-element.19), channel_id=1, source_target_pairs={{0,256},{16,272},{32,288},{48,304},{64,320},{80,336},{96,352},{112... | collective-permute-start | bytes 196616 | tf_op jit(solution)/shard_map/ppermute | solution.py:25
  149.7 0.8 copy-start
  149.7 1.0 copy-start.1

commit v2 on v0

v2 whole, which is shorter than its diff:
```python
import jax
import jax.numpy as jnp
from jax import lax
from jax.experimental import pallas as pl
from jax.experimental.pallas import tpu as pltpu
from jax.sharding import PartitionSpec as P

F32 = jnp.float32
BF16 = jnp.bfloat16
HALO = 2
SPREAD = 50.0
LOG2E = 1.4426950408889634
EXTRA = 64
BLK = 8

def pieces(x):
    a=x.astype(BF16).astype(F32); y=x-a
    b=y.astype(BF16).astype(F32)
    return a,b,y-b
def call(kernel, outs, scratch, prefetch, args, specs=None, alias=None):
    vmem = pl.BlockSpec(memory_space=pltpu.VMEM)
    smem = pl.BlockSpec(memory_space=pltpu.SMEM)
    return pl.pallas_call(kernel,
        out_shape=tuple(jax.ShapeDtypeStruct(s, F32) for s in outs),
        in_specs=[smem] * prefetch + (specs or [vmem] * (len(args) - prefetch)),
        out_specs=tuple([vmem] * len(outs)),
        scratch_shapes=scratch, input_output_aliases=alias or {},
        compiler_params=pltpu.CompilerParams(vmem_limit_bytes=56<<20))(*args)

def edge_kernel(first, last, points, order, up, down):
    n = first.shape[0]
    for out, rows, at in ((up, last, order.shape[1] - n), (down, first, 0)):
        out[:n, :] = rows[...]
        for c in range(3):
            for h in range(16):
                out[n + 16 * c + h : n + 16 * c + h + 1, :] = points[c : c + 1, 128 * h : 128 * h + 128]
        for h in range(n // 128):
            out[n + 48 + h : n + 49 + h, :] = order[:, at + 128 * h : at + 128 * h + 128].astype(F32)
        out[n + 48 + n // 128 :, :] = jnp.zeros((16 - n // 128, 128), F32)

def table_of(rows48):
    return jnp.concatenate(pieces(rows48), axis=0).astype(BF16)

def gathered(table, order_row):
    low = order_row & 127
    high = order_row >> 7
    hot = (lax.broadcasted_iota(jnp.int32, (128, 128), 0) == low).astype(F32).astype(BF16)
    r = jnp.dot(table, hot, preferred_element_type=F32)
    r = (r[0:48] + r[48:96]) + r[96:144]
    pick = lax.broadcasted_iota(jnp.int32, (16, 128), 0) == high
    return [jnp.sum(jnp.where(pick, r[16 * c : 16 * c + 16], 0.0), axis=0, keepdims=True) for c in range(3)]

def split_into(parts, w, block):
    high = block.astype(BF16)
    parts[w, :, :128] = high
    parts[w, :, 128:] = (block - high.astype(F32)).astype(BF16)

def spread_rows(points, rows, i):
    t = points[i].T
    for c in range(3):
        rows[i, c] = jnp.broadcast_to(t[:, c : c + 1], (256, 128))

def tile(rows, i, points, parts, w):
    cols = points[w]
    halves = []
    for g in range(2):
        d = None
        for c in range(3):
            e = rows[i, c] - cols[c : c + 1, 128 * g : 128 * g + 128]
            d = e * e if d is None else d + e * e
        halves.append(jnp.exp2(d * (-SPREAD * LOG2E)))
    kernel = jnp.concatenate(halves, axis=1)
    high = kernel.astype(BF16)
    low = (kernel - high.astype(F32)).astype(BF16)
    both = parts[w]
    out = jnp.dot(high, both, preferred_element_type=F32) + jnp.dot(low, both, preferred_element_type=F32)
    return out[:, :128] + out[:, 128:]

def list_tiles(near, counts, leaf_of, col_of, wanted, start):
    leaves = counts.shape[0]
    def leaf(i, n):
        def one(k, n):
            w = near[i, k]
            leaf_of[n] = i
            col_of[n] = w
            return n + jnp.where(wanted(w), 1, 0).astype(jnp.int32)
        return lax.fori_loop(0, counts[i], one, n)
    n = lax.fori_loop(0, leaves, leaf, start)
    return n

def run_tiles(n, leaf_of, col_of, at, y, spare, rows, points, parts, width=2):
    leaf_of_pad = spare
    for e in range(width):
        leaf_of[n + e] = spare
        col_of[n + e] = at
    def step(s, c):
        ids = [(leaf_of[s * width + e], col_of[s * width + e] - at) for e in range(width)]
        outs = [tile(rows, jnp.minimum(i, spare - 1), points, parts, w) for i, w in ids]
        for (i, _), o in zip(ids, outs):
            y[i] = y[i] + o
        return c
    lax.fori_loop(0, (n + width - 1) // width, step, 0)

def own_kernel(near, counts, raw, order, own, y_ref, p_ref, acc, parts, rows, tab, leaf_of, col_of):
    leaves = counts.shape[0]
    for c in range(3):
        for h in range(16):
            tab[16 * c + h : 16 * c + h + 1, :] = raw[c : c + 1, 128 * h : 128 * h + 128]
    table = table_of(tab[...])
    for h in range(2 * leaves):
        got = gathered(table, order[:, 128 * h : 128 * h + 128])
        for c in range(3):
            p_ref[h // 2, c : c + 1, 128 * (h % 2) : 128 * (h % 2) + 128] = got[c]
    for i in range(leaves):
        split_into(parts, i, own[256 * i : 256 * i + 256, :])
        p_ref[i, 3:8, :] = jnp.zeros((5, 256), F32)
        spread_rows(p_ref, rows, i)
        leaf_of[i] = i
        col_of[i] = HALO + i
        acc[i] = jnp.zeros((256, 128), F32)
    acc[leaves] = jnp.zeros((256, 128), F32)
    n = list_tiles(near, counts, leaf_of, col_of, lambda w: (w >= HALO) & (w < HALO + leaves), leaves)
    run_tiles(n, leaf_of, col_of, HALO, acc, leaves, rows, p_ref, parts)
    y_ref[...] = acc[:leaves]

def halo_kernel(near, counts, before, after, y_in, p_in, y_ref, g_ref, acc, parts, rows, points, leaf_of, col_of):
    leaves = counts.shape[0]
    n_edge = HALO * 256
    for side, src in ((0, before), (1, after)):
        table = table_of(src[n_edge : n_edge + 48, :])
        for h in range(2 * HALO):
            got = gathered(table, src[n_edge + 48 + h : n_edge + 49 + h, :].astype(jnp.int32))
            for c in range(3):
                points[side * HALO + h // 2, c : c + 1, 128 * (h % 2) : 128 * (h % 2) + 128] = got[c]
        for w in range(HALO):
            split_into(parts, side * HALO + w, src[256 * w : 256 * w + 256, :])
    for i in range(leaves):
        spread_rows(p_in, rows, i)
        acc[i] = y_in[i]
    acc[leaves] = jnp.zeros((256, 128), F32)
    n = list_tiles(near, counts, leaf_of, col_of, lambda w: (w < HALO) | (w >= HALO + leaves), 0)
    def fix(t, c):
        w = col_of[t]
        col_of[t] = jnp.where(w < HALO, w, w - leaves)
        return c
    lax.fori_loop(0, n, fix, 0)
    run_tiles(n, leaf_of, col_of, 0, acc, leaves, rows, points, parts)
    for i in range(leaves):
        y = acc[i]
        y_ref[i] = y
        b1, b2, b3 = [p.astype(BF16) for p in pieces(y)]
        b12 = jnp.concatenate([b1, b2], axis=1)
        q = jnp.dot(b12.T, b12, preferred_element_type=F32)
        q = (q[:128] + q[128:])
        t = jnp.dot(b1.T, b3, preferred_element_type=F32) + jnp.dot(b3.T, b1, preferred_element_type=F32)
        g_ref[i] = (q[:, :128] + q[:, 128:]) + t
    at, n = 0, leaves
    while n > 1:
        for c in range(n // 2):
            g_ref[at + n + c] = g_ref[at + 2 * c] + g_ref[at + 2 * c + 1]
        at += n
        n //= 2

def edge_blocks(points, order, samples):
    n = HALO * 256
    total = samples.shape[0] // n
    specs = [pl.BlockSpec((n, 128), lambda i: (0, 0)), pl.BlockSpec((n, 128), lambda i: (total - 1, 0)),
             pl.BlockSpec(points.shape, lambda i: (0, 0)), pl.BlockSpec(order.shape, lambda i: (0, 0))]
    o = pl.BlockSpec((n + EXTRA, 128), lambda i: (0, 0))
    return pl.pallas_call(edge_kernel, grid=(1,), in_specs=specs, out_specs=(o, o),
        out_shape=(jax.ShapeDtypeStruct((n + EXTRA, 128), F32),) * 2)(samples, samples, points, order)
def own_samples(near, counts, points, order, samples):
    L = counts.shape[0]
    return call(own_kernel, [(L,256,128),(L,8,256)],
        [pltpu.VMEM((L+1,256,128),F32), pltpu.VMEM((L,256,256),BF16), pltpu.VMEM((L,3,256,128),F32), pltpu.VMEM((48,128),F32), pltpu.SMEM((64,),jnp.int32), pltpu.SMEM((64,),jnp.int32)],
        2, (near, counts, points, order, samples))
def halo_samples(near, counts, before, after, y, p):
    L = counts.shape[0]
    return call(halo_kernel, [(L,256,128),(2*L-1,128,128)],
        [pltpu.VMEM((L+1,256,128),F32), pltpu.VMEM((2*HALO,256,256),BF16), pltpu.VMEM((L,3,256,128),F32), pltpu.VMEM((2*HALO,8,256),F32), pltpu.SMEM((64,),jnp.int32), pltpu.SMEM((64,),jnp.int32)],
        2, (near, counts, before, after, y, p))


def passed_along(block, axis, distance):
    devices = range(lax.axis_size(axis))
    route = [(i - distance, i) for i in devices if i - distance in devices]
    return lax.ppermute(block, axis, route)


def exchanged(value, axis, mask):
    return lax.ppermute(value, axis, [(i, i ^ mask) for i in range(lax.axis_size(axis))])


def row_of(x, j):
    return jnp.broadcast_to(x[j : j + 1, :], x.shape)


def factor_all(work, upper_out, inverse_out, groups):
    lane = lax.broadcasted_iota(jnp.int32, (BLK, 128), 1)
    sub = lax.broadcasted_iota(jnp.int32, (BLK, 128), 0)
    for k in range(128 // BLK):
        r = BLK * k
        on_diag = (lane >= r) & (lane < r + BLK)
        for group in groups:
            panel = {m: work[m, r : r + BLK, :] for m in group}
            diag = None
            for s, m in enumerate(group):
                shift = (BLK * s - r) % 128
                x = pltpu.roll(panel[m], shift, 1) if shift else panel[m]
                diag = x if s == 0 else jnp.where((lane >= BLK * s) & (lane < BLK * s + BLK), x, diag)
            cols = [pltpu.roll(diag, 128 - j, 1) if j else diag for j in range(BLK)]
            inv = [jnp.where(sub == j, 1.0, 0.0).astype(F32) for j in range(BLK)]
            scale = jnp.ones((BLK, 128), F32)
            for j in range(BLK):
                below = jnp.where(sub > j, cols[j], 0.0)
                rs = lax.rsqrt(row_of(cols[j], j))
                mult = below * rs
                for q in range(j + 1, BLK):
                    cols[q] = cols[q] - mult * (row_of(cols[q], j) * rs)
                for q in range(j + 1):
                    inv[q] = inv[q] - mult * (row_of(inv[q], j) * rs)
                scale = jnp.where(sub == j, rs, scale)
            inv = [e * scale for e in inv]
            for s, m in enumerate(group):
                out = block = None
                for q in range(BLK):
                    x = jnp.broadcast_to(inv[q][:, BLK * s : BLK * s + 1], (BLK, 128))
                    t = x * row_of(panel[m], q)
                    out = t if q == 0 else out + t
                    block = x if q == 0 else jnp.where(lane == r + q, x, block)
                upper_out[m, r : r + BLK, :] = jnp.where(lane >= r + sub, out, 0.0)
                right = jnp.where(on_diag, block, out)
                inverse_out[m, r : r + BLK, :] = jnp.where(lane < r + BLK, right, 0.0)
                if r + BLK < 128:
                    p1, p2, p3 = pieces(right)
                    rhs = jnp.concatenate([p1, p2, p1, p2, p3, p1], axis=0).astype(BF16)
                    lhs = jnp.concatenate([p1, p1, p2, p2, p1, p3], axis=0).astype(BF16)
                    update = jnp.dot(lhs.T[r + BLK :], rhs, preferred_element_type=F32)
                    at = lax.broadcasted_iota(jnp.int32, (128 - r - BLK, 128), 1)
                    old = work[m, r + BLK :, :]
                    work[m, r + BLK :, :] = jnp.where((at >= r) & (at < r + BLK), 0.0, old) - update


def times_transposed(x, y):
    return lax.dot_general(
        x, y, (((1,), (1,)), ((), ())), precision=lax.Precision.HIGHEST, preferred_element_type=F32
    )


def local_factor_kernel(g_ref, upper_ref, inverse_ref, work):
    work[...] = g_ref[...]
    factor_all(work, upper_ref, inverse_ref, [list(range(g_ref.shape[0]))])


def local_basis_kernel(y_ref, upper_ref, inverse_ref, leaf_ref, base_ref):
    leaves = y_ref.shape[0]
    for m in range(leaves):
        leaf_ref[m * 256 : m * 256 + 256, :] = times_transposed(y_ref[m], inverse_ref[m])
    for n in range(leaves - 1):
        for half in range(2):
            base_ref[n, half * 128 : half * 128 + 128, :] = times_transposed(
                upper_ref[2 * n + half], inverse_ref[leaves + n]
            )


def upper_kernel(low_bits, *refs):
    levels = (len(refs) - 6) // 2
    first = refs[0]
    own = refs[1 : 1 + levels]
    partner = refs[1 + levels : 1 + 2 * levels]
    base_ref, root_ref, work, upper, inverse = refs[1 + 2 * levels :]
    place = (lax.axis_index("tx") << low_bits) + lax.axis_index("ty")
    for m in range(levels):
        work[m] = own[m][...]
        work[levels + m] = partner[m][...]
    factor_all(work, upper, inverse, [list(range(levels)), list(range(levels, 2 * levels))])
    for h in range(levels):
        mine = first[...] if h == 0 else upper[h - 1]
        a = times_transposed(mine, inverse[h])
        b = times_transposed(upper[levels + h], inverse[h])
        bit = (place >> h) & 1
        base_ref[h, pl.ds(bit * 128, 128), :] = a
        base_ref[h, pl.ds((1 - bit) * 128, 128), :] = b
    root_ref[...] = upper[levels - 1]


def per_device(points, tree_order, samples, near_leaves, near_counts):
    leaves = near_counts.shape[0]
    nodes = 2 * leaves - 1
    both = ("tx", "ty")
    for_after, for_before = edge_blocks(points, tree_order, samples)
    before = passed_along(for_after, both, 1)
    after = passed_along(for_before, both, -1)
    part, ordered = own_samples(near_leaves, near_counts, points, tree_order, samples)
    sampled, grams = halo_samples(near_leaves, near_counts, before, after, part, ordered)
    gram = grams[nodes - 1]
    owns, partners = [], []
    low_bits = lax.axis_size("ty").bit_length() - 1
    high_bits = lax.axis_size("tx").bit_length() - 1
    steps = [("ty", m) for m in [1, 2, 4, 15]] + [("tx", m) for m in [1, 2, 6, 8, 24]]
    assert [m.bit_length() for _, m in steps] == [*range(1, low_bits + 1), *range(1, high_bits + 1)]
    for h, (axis, mask) in enumerate(steps):
        if h == 2:
            grams, gram = lax.optimization_barrier((grams, gram))
        if h == 3:
            sampled, gram = lax.optimization_barrier((sampled, gram))
        partner = exchanged(gram, axis, mask)
        if h == 2:
            uppers, inverses = call(
                local_factor_kernel, [(nodes, 128, 128)] * 2, [pltpu.VMEM((nodes, 128, 128), F32)], 0, (grams,)
            )
            partner, uppers, inverses = lax.optimization_barrier((partner, uppers, inverses))
        if h == 3:
            leaf_bases, local_bases = call(
                local_basis_kernel,
                [(leaves * 256, 128), (leaves - 1, 256, 128)],
                [],
                0,
                (sampled, uppers, inverses),
            )
            partner, leaf_bases, local_bases = lax.optimization_barrier((partner, leaf_bases, local_bases))
        gram = gram + partner
        owns.append(gram)
        partners.append(partner)
    levels = len(owns)
    upper_bases, root = call(
        lambda *refs: upper_kernel(low_bits, *refs),
        [(levels, 256, 128), (128, 128)],
        [pltpu.VMEM((2 * levels, 128, 128), F32)] * 3,
        0,
        (uppers[nodes - 1], *owns, *partners),
    )
    return leaf_bases, local_bases, upper_bases, root


def solution(mesh):
    return jax.shard_map(
        per_device,
        mesh=mesh,
        in_specs=(
            P(None, ("tx", "ty")),
            P(("tx", "ty"), None),
            P(("tx", "ty"), None),
            P(("tx", "ty"), None),
            P(("tx", "ty")),
        ),
        out_specs=(
            P(("tx", "ty"), None),
            P(("tx", "ty"), None, None),
            P(("tx", "ty"), None, None),
            P(),
        ),
        check_vma=False,
    )
```

time: 703 us -> 129 us (0.18)
  other arithmetic: 538 us -> 1.57 us
  Pallas kernels: 0 us -> 54.9 us
  matrix products: 35.1 us -> 0 us
  local copies, waits for them, and re-layouts: 25.4 us -> 3.15 us
  waiting for transfers between devices: 46.3 us -> 28.4 us
  starting transfers between devices: 52.4 us -> 39 us
    another operation x57 -> x0, other arithmetic: 527 us -> none  [the longest x40 289 us: orthonormalize(): lower_factor = jnp.linalg.cholesky(gram_matrix)]
    pallas_call x0 -> x6, Pallas kernels: none -> 54.9 us  [the longest x5 53 us: call(): pl.pallas_call(kernel, out_shape=tuple((jax.ShapeDtypeStruct(s, F32) for...]
    dot_general x19 -> x0, matrix products: 29 us -> none  [the longest x6 22.7 us: kernel_tile(): jnp.einsum('lij,ljr->lir', kernel, column_samples, precision=lax.Precisio...]
    gather x11 -> x0, local copies, waits for them, and re-layouts: 16.4 us -> none  [the longest x5 8.01 us: per_device(): jnp.take(window_samples, column_leaf, axis=0)]
    ppermute x9, waiting for transfers between devices: 38.6 us -> 28.4 us  [exchanged(): lax.ppermute(value, axis, [(i, i ^ mask) for i in range(lax.axis_size(axi...]
    ppermute x4 -> x2, starting transfers between devices: 24.9 us -> 15.1 us  [passed_along(): return lax.ppermute(block, axis, route)]
    ppermute x4 -> x2, waiting for transfers between devices: 7.67 us -> 0.01 us  [passed_along(): return lax.ppermute(block, axis, route)]
  transfers between devices with their start and end apart: 13 -> 11, of which waited for: 10 -> 7; matrix products, arithmetic and copies ran while one was open for 3% -> 1% of each run, Pallas kernels for 0% -> 23%
where the time goes in v2:
time: 129 us; the launch traced here: 128 us
  Pallas kernels  54.9 us (43%)
  starting transfers between devices  39 us (30%)
  waiting for transfers between devices  28.4 us (22%)
  local copies, waits for them, and re-layouts  3.15 us (2%)
  other arithmetic  1.57 us (1%)
    pallas_call x5, Pallas kernels, call(): pl.pallas_call(kernel, out_shape=tuple((jax.ShapeDtypeStruct(s, F32) for...  53 us
    ppermute x9, waiting for transfers between devices, exchanged(): lax.ppermute(value, axis, [(i, i ^ mask) for i in range(lax.axis_size(axi...  28.4 us
    ppermute x9, starting transfers between devices, exchanged(): lax.ppermute(value, axis, [(i, i ^ mask) for i in range(lax.axis_size(axi...  23.9 us
    ppermute x2, starting transfers between devices, passed_along(): return lax.ppermute(block, axis, route)  15.1 us
  transfers between devices with their start and end apart: 11, of which 7 were waited for; matrix products, arithmetic and copies ran while one was open for 1% of the time, Pallas kernels for 23%

profile of v2, /device:TPU:24, one launch (start us, length us, event | category | flops | bytes accessed | tf_op | source)
XLA Modules:
  0.0 128.0 jit_solution(383308167035721910)
XLA Ops:
  0.6 1.9 %shard_map.84 = (f32[576,128]{1,0:T(8,128)}, f32[576,128]{1,0:T(8,128)}) custom-call(f32[2048,128]{1,0:T(8,128)} %own.1, f32[2048,128]{1,0:T(8,128)} %own.1, f32[3,2048]{1,0:T(4,128)} %raw.1, s32[1,2048]{1,0:T(1,128)} %order.3), custom_call_target="tpu_custom_call" | custom-call | tf_op jit(solution)/shard_map/pallas_call | solution.py:170
  2.5 3.8 %collective-permute-start = (f32[576,128]{1,0:T(8,128)}, f32[576,128]{1,0:T(8,128)S(1)}, u32[]{:S(2)}, u32[]{:S(2)}) collective-permute-start(f32[576,128]{1,0:T(8,128)} %get-tuple-element.26), channel_id=1, source_target_pairs={{0,1},{1,2},{2,3},{3,4},{4,5},{5,6},{6,7},{7,8},{8,9},{9,10},{10,1... | collective-permute-start | bytes 884744 | tf_op jit(solution)/shard_map/ppermute | solution.py:187
  6.3 11.3 %collective-permute-start.1 = (f32[576,128]{1,0:T(8,128)}, f32[576,128]{1,0:T(8,128)S(1)}, u32[]{:S(2)}, u32[]{:S(2)}) collective-permute-start(f32[576,128]{1,0:T(8,128)} %get-tuple-element.27), channel_id=1, source_target_pairs={{1,0},{2,1},{3,2},{4,3},{5,4},{6,5},{7,6},{8,7},{9,8},{10,9},{11,1... | collective-permute-start | bytes 884744 | tf_op jit(solution)/shard_map/ppermute | solution.py:187
  17.7 9.6 %shard_map.85 = (f32[8,256,128]{2,1,0:T(8,128)}, f32[8,8,256]{2,1,0:T(8,128)}) custom-call(s32[8,5]{1,0:T(8,128)} %near.3, s32[8]{0:T(128)} %counts.3, f32[3,2048]{1,0:T(4,128)} %raw.1, s32[1,2048]{1,0:T(1,128)} %order.3, f32[2048,128]{1,0:T(8,128)} %own.1), custom_call_target="tpu_custom_call" | custom-call | tf_op jit(solution)/shard_map/pallas_call | solution.py:23
  27.3 0.0 collective-permute-done.before
  27.3 0.0 collective-permute-done.1.after
  27.3 0.0 copy-start.9
  27.3 0.7 copy-done.8
  28.0 0.1 copy-done.9
  28.1 7.2 %shard_map.86 = (f32[8,256,128]{2,1,0:T(8,128)}, f32[15,128,128]{2,1,0:T(8,128)}) custom-call(s32[8,5]{1,0:T(8,128)} %near.3, s32[8]{0:T(128)} %counts.3, f32[576,128]{1,0:T(8,128)} %copy-done.8, f32[576,128]{1,0:T(8,128)} %copy-done.9, f32[8,256,128]{2,1,0:T(8,128)} %get-tuple-element.28.y_in, f32[8,8,256]{2,1,0:T(8,128)} %get-tuple-element.29.p_in), custom_call_target="tpu_custom_call" | custom-call | tf_op jit(solution)/shard_map/pallas_call | solution.py:23
  35.3 0.8 slice_bitcast_fusion.1
  36.1 1.9 %collective-permute-start.2 = (f32[128,128]{1,0:T(8,128)S(1)}, f32[128,128]{1,0:T(8,128)S(1)}, u32[]{:S(2)}, u32[]{:S(2)}) collective-permute-start(f32[128,128]{1,0:T(8,128)S(1)} %slice_bitcast_fusion.1), channel_id=1, source_target_pairs={{0,1},{1,0},{2,3},{3,2},{4,5},{5,4},{6,7},{7,6},{8,9},{9,8},{10,11... | collective-permute-start | bytes 196616 | tf_op jit(solution)/shard_map/ppermute | solution.py:191
  38.0 4.2 %collective-permute-done.2.refs_10_ = f32[128,128]{1,0:T(8,128)S(1)} collective-permute-done((f32[128,128]{1,0:T(8,128)S(1)}, f32[128,128]{1,0:T(8,128)S(1)}, u32[]{:S(2)}, u32[]{:S(2)}) %collective-permute-start.2) | collective-permute-done | bytes 65568 | tf_op jit(solution)/shard_map/ppermute | solution.py:191
  42.3 0.9 fusion.refs_1_
  43.1 1.9 %collective-permute-start.3 = (f32[128,128]{1,0:T(8,128)S(1)}, f32[128,128]{1,0:T(8,128)S(1)}, u32[]{:S(2)}, u32[]{:S(2)}) collective-permute-start(f32[128,128]{1,0:T(8,128)S(1)} %fusion.refs_1_), channel_id=1, source_target_pairs={{0,2},{1,3},{2,0},{3,1},{4,6},{5,7},{6,4},{7,5},{8,10},{9,11},{10,... | collective-permute-start | bytes 196616 | tf_op jit(solution)/shard_map/ppermute | solution.py:191
  45.1 5.3 %collective-permute-done.3.refs_11_ = f32[128,128]{1,0:T(8,128)S(1)} collective-permute-done((f32[128,128]{1,0:T(8,128)S(1)}, f32[128,128]{1,0:T(8,128)S(1)}, u32[]{:S(2)}, u32[]{:S(2)}) %collective-permute-start.3) | collective-permute-done | bytes 65568 | tf_op jit(solution)/shard_map/ppermute | solution.py:191
  50.4 0.0 copy-start.1
  50.4 2.1 %collective-permute-start.4 = (f32[128,128]{1,0:T(8,128)S(1)}, f32[128,128]{1,0:T(8,128)S(1)}, u32[]{:S(2)}, u32[]{:S(2)}) collective-permute-start(f32[128,128]{1,0:T(8,128)S(1)} %add.28.refs_2_), channel_id=1, source_target_pairs={{0,4},{1,5},{2,6},{3,7},{4,0},{5,1},{6,2},{7,3},{8,12},{9,13},{10,... | collective-permute-start | bytes 196616 | tf_op jit(solution)/shard_map/ppermute | solution.py:191
  52.5 14.6 %shard_map.87 = (f32[15,128,128]{2,1,0:T(8,128)}, f32[15,128,128]{2,1,0:T(8,128)}) custom-call(f32[15,128,128]{2,1,0:T(8,128)} %get-tuple-element.33.g_ref), custom_call_target="tpu_custom_call" | custom-call | tf_op jit(solution)/shard_map/pallas_call | solution.py:23
  67.1 0.0 collective-permute-done.4.refs_12_
  67.1 0.0 copy-start.2
  67.1 8.1 %collective-permute-start.5 = (f32[128,128]{1,0:T(8,128)S(1)}, f32[128,128]{1,0:T(8,128)S(1)}, u32[]{:S(2)}, u32[]{:S(2)}) collective-permute-start(f32[128,128]{1,0:T(8,128)S(1)} %add.29.refs_3_), channel_id=1, source_target_pairs={{0,15},{1,14},{2,13},{3,12},{4,11},{5,10},{6,9},{7,8},{8,7},{9,6},... | collective-permute-start | bytes 196616 | tf_op jit(solution)/shard_map/ppermute | solution.py:191
  75.3 5.6 %shard_map.88 = (f32[2048,128]{1,0:T(8,128)}, f32[7,256,128]{2,1,0:T(8,128)}) custom-call(f32[8,256,128]{2,1,0:T(8,128)} %get-tuple-element.38.y_ref, f32[15,128,128]{2,1,0:T(8,128)} %get-tuple-element.39.upper_ref, f32[15,128,128]{2,1,0:T(8,128)} %get-tuple-element.40.inverse_ref), custom_call_target="tpu_custom_call" | custom-call | tf_op jit(solution)/shard_map/pallas_call | solution.py:23
  80.9 0.0 copy-done.10
  80.9 0.0 collective-permute-done.5.refs_13_
  81.0 1.9 %collective-permute-start.6 = (f32[128,128]{1,0:T(8,128)S(1)}, f32[128,128]{1,0:T(8,128)S(1)}, u32[]{:S(2)}, u32[]{:S(2)}) collective-permute-start(f32[128,128]{1,0:T(8,128)S(1)} %add.30.refs_4_), channel_id=1, source_target_pairs={{0,16},{16,0},{32,48},{48,32},{64,80},{80,64},{96,112},{112,96},{1... | collective-permute-start | bytes 196616 | tf_op jit(solution)/shard_map/ppermute | solution.py:191
  82.9 1.2 collective-permute-done.6.refs_14_
  84.1 0.0 copy-start.4
  84.1 1.9 %collective-permute-start.7 = (f32[128,128]{1,0:T(8,128)S(1)}, f32[128,128]{1,0:T(8,128)S(1)}, u32[]{:S(2)}, u32[]{:S(2)}) collective-permute-start(f32[128,128]{1,0:T(8,128)S(1)} %add.31.refs_5_), channel_id=1, source_target_pairs={{0,32},{16,48},{32,0},{48,16},{64,96},{80,112},{96,64},{112,80},{1... | collective-permute-start | bytes 196616 | tf_op jit(solution)/shard_map/ppermute | solution.py:191
  86.1 4.2 %collective-permute-done.7.refs_15_ = f32[128,128]{1,0:T(8,128)S(1)} collective-permute-done((f32[128,128]{1,0:T(8,128)S(1)}, f32[128,128]{1,0:T(8,128)S(1)}, u32[]{:S(2)}, u32[]{:S(2)}) %collective-permute-start.7) | collective-permute-done | bytes 65568 | tf_op jit(solution)/shard_map/ppermute | solution.py:191
  90.3 1.9 %collective-permute-start.8 = (f32[128,128]{1,0:T(8,128)S(1)}, f32[128,128]{1,0:T(8,128)S(1)}, u32[]{:S(2)}, u32[]{:S(2)}) collective-permute-start(f32[128,128]{1,0:T(8,128)S(1)} %add.32.refs_6_), channel_id=1, source_target_pairs={{0,96},{16,112},{32,64},{48,80},{64,32},{80,48},{96,0},{112,16},{1... | collective-permute-start | bytes 196616 | tf_op jit(solution)/shard_map/ppermute | solution.py:191
  92.2 5.4 %collective-permute-done.8.refs_16_ = f32[128,128]{1,0:T(8,128)S(1)} collective-permute-done((f32[128,128]{1,0:T(8,128)S(1)}, f32[128,128]{1,0:T(8,128)S(1)}, u32[]{:S(2)}, u32[]{:S(2)}) %collective-permute-start.8) | collective-permute-done | bytes 65568 | tf_op jit(solution)/shard_map/ppermute | solution.py:191
  97.7 0.0 copy-start.6
  97.7 1.9 %collective-permute-start.9 = (f32[128,128]{1,0:T(8,128)S(1)}, f32[128,128]{1,0:T(8,128)S(1)}, u32[]{:S(2)}, u32[]{:S(2)}) collective-permute-start(f32[128,128]{1,0:T(8,128)S(1)} %add.33.refs_7_), channel_id=1, source_target_pairs={{0,128},{16,144},{32,160},{48,176},{64,192},{80,208},{96,224},{112... | collective-permute-start | bytes 196616 | tf_op jit(solution)/shard_map/ppermute | solution.py:191
  99.6 4.2 %collective-permute-done.9.refs_17_ = f32[128,128]{1,0:T(8,128)S(1)} collective-permute-done((f32[128,128]{1,0:T(8,128)S(1)}, f32[128,128]{1,0:T(8,128)S(1)}, u32[]{:S(2)}, u32[]{:S(2)}) %collective-permute-start.9) | collective-permute-done | bytes 65568 | tf_op jit(solution)/shard_map/ppermute | solution.py:191
  103.9 2.1 %collective-permute-start.10 = (f32[128,128]{1,0:T(8,128)S(1)}, f32[128,128]{1,0:T(8,128)S(1)}, u32[]{:S(2)}, u32[]{:S(2)}) collective-permute-start(f32[128,128]{1,0:T(8,128)S(1)} %add.34.refs_8_), channel_id=1, source_target_pairs={{0,384},{16,400},{32,416},{48,432},{64,448},{80,464},{96,480},{112... | collective-permute-start | bytes 196616 | tf_op jit(solution)/shard_map/ppermute | solution.py:191
  106.0 1.5 %slice_bitcast_fusion.refs_0_ = f32[128,128]{1,0:T(8,128)} fusion(f32[15,128,128]{2,1,0:T(8,128)} %get-tuple-element.39.upper_ref), kind=kLoop, calls=%fused_computation | loop fusion | bytes 131072 | tf_op jit(solution)/shard_map/squeeze | solution.py:331
  107.5 3.8 %collective-permute-done.10.refs_18_ = f32[128,128]{1,0:T(8,128)S(1)} collective-permute-done((f32[128,128]{1,0:T(8,128)S(1)}, f32[128,128]{1,0:T(8,128)S(1)}, u32[]{:S(2)}, u32[]{:S(2)}) %collective-permute-start.10) | collective-permute-done | bytes 65568 | tf_op jit(solution)/shard_map/ppermute | solution.py:191
  111.3 0.6 add.35.refs_9_
  111.9 0.0 copy-done.4
  111.9 0.0 copy-done.15
  111.9 0.0 copy-done.5
  111.9 0.0 copy-done.16
  112.0 0.0 copy-done.6
  112.0 0.0 copy-done.17
  112.0 0.0 copy-done.7
  112.0 0.0 copy-done.18
  112.0 16.0 %shard_map.89 = (f32[9,256,128]{2,1,0:T(8,128)}, f32[128,128]{1,0:T(8,128)}) custom-call(f32[128,128]{1,0:T(8,128)} %slice_bitcast_fusion.refs_0_, f32[128,128]{1,0:T(8,128)} %copy-done, f32[128,128]{1,0:T(8,128)} %copy-done.1, f32[128,128]{1,0:T(8,128)} %copy-done.2, f32[128,128]{1,0:T(8,128)} %copy-done.3, f32[128,128]{1,0:T(8,128)} %copy-done.4, ...), custom_call_target="tpu_custom_call" | custom-call | tf_op jit(solution)/shard_map/pallas_call | solution.py:23
  (29 shorter events, 0.1 us)
Async XLA Ops:
  2.5 24.7 %collective-permute-start = (f32[576,128]{1,0:T(8,128)}, f32[576,128]{1,0:T(8,128)S(1)}, u32[]{:S(2)}, u32[]{:S(2)}) collective-permute-start(f32[576,128]{1,0:T(8,128)} %get-tuple-element.26), channel_id=1, source_target_pairs={{0,1},{1,2},{2,3},{3,4},{4,5},{5,6},{6,7},{7,8},{8,9},{9,10},{10,1... | collective-permute-start | bytes 884744 | tf_op jit(solution)/shard_map/ppermute | solution.py:187
  6.3 20.9 %collective-permute-start.1 = (f32[576,128]{1,0:T(8,128)}, f32[576,128]{1,0:T(8,128)S(1)}, u32[]{:S(2)}, u32[]{:S(2)}) collective-permute-start(f32[576,128]{1,0:T(8,128)} %get-tuple-element.27), channel_id=1, source_target_pairs={{1,0},{2,1},{3,2},{4,3},{5,4},{6,5},{7,6},{8,7},{9,8},{10,9},{11,1... | collective-permute-start | bytes 884744 | tf_op jit(solution)/shard_map/ppermute | solution.py:187
  27.3 0.7 copy-start.8
  27.3 0.8 copy-start.9
  36.1 6.1 %collective-permute-start.2 = (f32[128,128]{1,0:T(8,128)S(1)}, f32[128,128]{1,0:T(8,128)S(1)}, u32[]{:S(2)}, u32[]{:S(2)}) collective-permute-start(f32[128,128]{1,0:T(8,128)S(1)} %slice_bitcast_fusion.1), channel_id=1, source_target_pairs={{0,1},{1,0},{2,3},{3,2},{4,5},{5,4},{6,7},{7,6},{8,9},{9,8},{10,11... | collective-permute-start | bytes 196616 | tf_op jit(solution)/shard_map/ppermute | solution.py:191
  42.3 38.6 %copy-start.10 = (f32[128,128]{1,0:T(8,128)}, f32[128,128]{1,0:T(8,128)S(1)}, u32[]{:S(2)}) copy-start(f32[128,128]{1,0:T(8,128)S(1)} %collective-permute-done.2.refs_10_) | copy-start | bytes 196612
  43.1 37.7 %copy-start = (f32[128,128]{1,0:T(8,128)}, f32[128,128]{1,0:T(8,128)S(1)}, u32[]{:S(2)}) copy-start(f32[128,128]{1,0:T(8,128)S(1)} %fusion.refs_1_) | copy-start | bytes 196612
  43.1 7.2 %collective-permute-start.3 = (f32[128,128]{1,0:T(8,128)S(1)}, f32[128,128]{1,0:T(8,128)S(1)}, u32[]{:S(2)}, u32[]{:S(2)}) collective-permute-start(f32[128,128]{1,0:T(8,128)S(1)} %fusion.refs_1_), channel_id=1, source_target_pairs={{0,2},{1,3},{2,0},{3,1},{4,6},{5,7},{6,4},{7,5},{8,10},{9,11},{10,... | collective-permute-start | bytes 196616 | tf_op jit(solution)/shard_map/ppermute | solution.py:191
  50.4 30.5 %copy-start.11 = (f32[128,128]{1,0:T(8,128)}, f32[128,128]{1,0:T(8,128)S(1)}, u32[]{:S(2)}) copy-start(f32[128,128]{1,0:T(8,128)S(1)} %collective-permute-done.3.refs_11_) | copy-start | bytes 196612
  50.4 30.5 %copy-start.1 = (f32[128,128]{1,0:T(8,128)}, f32[128,128]{1,0:T(8,128)S(1)}, u32[]{:S(2)}) copy-start(f32[128,128]{1,0:T(8,128)S(1)} %add.28.refs_2_) | copy-start | bytes 196612
  50.4 16.7 %collective-permute-start.4 = (f32[128,128]{1,0:T(8,128)S(1)}, f32[128,128]{1,0:T(8,128)S(1)}, u32[]{:S(2)}, u32[]{:S(2)}) collective-permute-start(f32[128,128]{1,0:T(8,128)S(1)} %add.28.refs_2_), channel_id=1, source_target_pairs={{0,4},{1,5},{2,6},{3,7},{4,0},{5,1},{6,2},{7,3},{8,12},{9,13},{10,... | collective-permute-start | bytes 196616 | tf_op jit(solution)/shard_map/ppermute | solution.py:191
  67.1 13.8 %copy-start.12 = (f32[128,128]{1,0:T(8,128)}, f32[128,128]{1,0:T(8,128)S(1)}, u32[]{:S(2)}) copy-start(f32[128,128]{1,0:T(8,128)S(1)} %collective-permute-done.4.refs_12_) | copy-start | bytes 196612
  67.1 13.8 %copy-start.2 = (f32[128,128]{1,0:T(8,128)}, f32[128,128]{1,0:T(8,128)S(1)}, u32[]{:S(2)}) copy-start(f32[128,128]{1,0:T(8,128)S(1)} %add.29.refs_3_) | copy-start | bytes 196612
  67.1 13.8 %collective-permute-start.5 = (f32[128,128]{1,0:T(8,128)S(1)}, f32[128,128]{1,0:T(8,128)S(1)}, u32[]{:S(2)}, u32[]{:S(2)}) collective-permute-start(f32[128,128]{1,0:T(8,128)S(1)} %add.29.refs_3_), channel_id=1, source_target_pairs={{0,15},{1,14},{2,13},{3,12},{4,11},{5,10},{6,9},{7,8},{8,7},{9,6},... | collective-permute-start | bytes 196616 | tf_op jit(solution)/shard_map/ppermute | solution.py:191
  80.9 31.0 %copy-start.13 = (f32[128,128]{1,0:T(8,128)}, f32[128,128]{1,0:T(8,128)S(1)}, u32[]{:S(2)}) copy-start(f32[128,128]{1,0:T(8,128)S(1)} %collective-permute-done.5.refs_13_) | copy-start | bytes 196612
  80.9 31.0 %copy-start.3 = (f32[128,128]{1,0:T(8,128)}, f32[128,128]{1,0:T(8,128)S(1)}, u32[]{:S(2)}) copy-start(f32[128,128]{1,0:T(8,128)S(1)} %add.30.refs_4_) | copy-start | bytes 196612
  81.0 3.1 %collective-permute-start.6 = (f32[128,128]{1,0:T(8,128)S(1)}, f32[128,128]{1,0:T(8,128)S(1)}, u32[]{:S(2)}, u32[]{:S(2)}) collective-permute-start(f32[128,128]{1,0:T(8,128)S(1)} %add.30.refs_4_), channel_id=1, source_target_pairs={{0,16},{16,0},{32,48},{48,32},{64,80},{80,64},{96,112},{112,96},{1... | collective-permute-start | bytes 196616 | tf_op jit(solution)/shard_map/ppermute | solution.py:191
  84.1 27.8 %copy-start.14 = (f32[128,128]{1,0:T(8,128)}, f32[128,128]{1,0:T(8,128)S(1)}, u32[]{:S(2)}) copy-start(f32[128,128]{1,0:T(8,128)S(1)} %collective-permute-done.6.refs_14_) | copy-start | bytes 196612
  84.1 27.8 %copy-start.4 = (f32[128,128]{1,0:T(8,128)}, f32[128,128]{1,0:T(8,128)S(1)}, u32[]{:S(2)}) copy-start(f32[128,128]{1,0:T(8,128)S(1)} %add.31.refs_5_) | copy-start | bytes 196612
  84.1 6.2 %collective-permute-start.7 = (f32[128,128]{1,0:T(8,128)S(1)}, f32[128,128]{1,0:T(8,128)S(1)}, u32[]{:S(2)}, u32[]{:S(2)}) collective-permute-start(f32[128,128]{1,0:T(8,128)S(1)} %add.31.refs_5_), channel_id=1, source_target_pairs={{0,32},{16,48},{32,0},{48,16},{64,96},{80,112},{96,64},{112,80},{1... | collective-permute-start | bytes 196616 | tf_op jit(solution)/shard_map/ppermute | solution.py:191
  90.3 21.6 %copy-start.15 = (f32[128,128]{1,0:T(8,128)}, f32[128,128]{1,0:T(8,128)S(1)}, u32[]{:S(2)}) copy-start(f32[128,128]{1,0:T(8,128)S(1)} %collective-permute-done.7.refs_15_) | copy-start | bytes 196612
  90.3 21.6 %copy-start.5 = (f32[128,128]{1,0:T(8,128)}, f32[128,128]{1,0:T(8,128)S(1)}, u32[]{:S(2)}) copy-start(f32[128,128]{1,0:T(8,128)S(1)} %add.32.refs_6_) | copy-start | bytes 196612
  90.3 7.4 %collective-permute-start.8 = (f32[128,128]{1,0:T(8,128)S(1)}, f32[128,128]{1,0:T(8,128)S(1)}, u32[]{:S(2)}, u32[]{:S(2)}) collective-permute-start(f32[128,128]{1,0:T(8,128)S(1)} %add.32.refs_6_), channel_id=1, source_target_pairs={{0,96},{16,112},{32,64},{48,80},{64,32},{80,48},{96,0},{112,16},{1... | collective-permute-start | bytes 196616 | tf_op jit(solution)/shard_map/ppermute | solution.py:191
  97.7 14.3 %copy-start.16 = (f32[128,128]{1,0:T(8,128)}, f32[128,128]{1,0:T(8,128)S(1)}, u32[]{:S(2)}) copy-start(f32[128,128]{1,0:T(8,128)S(1)} %collective-permute-done.8.refs_16_) | copy-start | bytes 196612
  97.7 14.2 %copy-start.6 = (f32[128,128]{1,0:T(8,128)}, f32[128,128]{1,0:T(8,128)S(1)}, u32[]{:S(2)}) copy-start(f32[128,128]{1,0:T(8,128)S(1)} %add.33.refs_7_) | copy-start | bytes 196612
  97.7 6.2 %collective-permute-start.9 = (f32[128,128]{1,0:T(8,128)S(1)}, f32[128,128]{1,0:T(8,128)S(1)}, u32[]{:S(2)}, u32[]{:S(2)}) collective-permute-start(f32[128,128]{1,0:T(8,128)S(1)} %add.33.refs_7_), channel_id=1, source_target_pairs={{0,128},{16,144},{32,160},{48,176},{64,192},{80,208},{96,224},{112... | collective-permute-start | bytes 196616 | tf_op jit(solution)/shard_map/ppermute | solution.py:191
  103.9 8.1 %copy-start.17 = (f32[128,128]{1,0:T(8,128)}, f32[128,128]{1,0:T(8,128)S(1)}, u32[]{:S(2)}) copy-start(f32[128,128]{1,0:T(8,128)S(1)} %collective-permute-done.9.refs_17_) | copy-start | bytes 196612
  103.9 8.1 %copy-start.7 = (f32[128,128]{1,0:T(8,128)}, f32[128,128]{1,0:T(8,128)S(1)}, u32[]{:S(2)}) copy-start(f32[128,128]{1,0:T(8,128)S(1)} %add.34.refs_8_) | copy-start | bytes 196612
  103.9 7.4 %collective-permute-start.10 = (f32[128,128]{1,0:T(8,128)S(1)}, f32[128,128]{1,0:T(8,128)S(1)}, u32[]{:S(2)}, u32[]{:S(2)}) collective-permute-start(f32[128,128]{1,0:T(8,128)S(1)} %add.34.refs_8_), channel_id=1, source_target_pairs={{0,384},{16,400},{32,416},{48,432},{64,448},{80,464},{96,480},{112... | collective-permute-start | bytes 196616 | tf_op jit(solution)/shard_map/ppermute | solution.py:191
  111.3 0.7 copy-start.18

commit v3 on v2

--- a/solution.py
+++ b/solution.py
@@ -75,6 +75,20 @@
     both = parts[w]
     out = jnp.dot(high, both, preferred_element_type=F32) + jnp.dot(low, both, preferred_element_type=F32)
     return out[:, :128] + out[:, 128:]
+
+def packed(g, out):
+    lane = lax.broadcasted_iota(jnp.int32, (1, 128), 1)
+    out[0:32, :] = g[0:32]
+    out[32:64, :] = jnp.where(lane < 32, pltpu.roll(g[96:128], 32, 1), g[32:64])
+    out[64:80, :] = jnp.where(lane < 64, pltpu.roll(g[80:96], 64, 1), g[64:80])
+
+
+def unpacked(p, out, m):
+    out[m, 0:64, :] = p[0:64, :]
+    out[m, 64:80, :] = p[64:80, :]
+    out[m, 80:96, :] = pltpu.roll(p[64:80, :], 64, 1)
+    out[m, 96:128, :] = pltpu.roll(p[32:64, :], 96, 1)
+
 
 def list_tiles(near, counts, leaf_of, col_of, wanted, start):
     leaves = counts.shape[0]
@@ -123,7 +137,7 @@
     run_tiles(n, leaf_of, col_of, HALO, acc, leaves, rows, p_ref, parts)
     y_ref[...] = acc[:leaves]
 
-def halo_kernel(near, counts, before, after, y_in, p_in, y_ref, g_ref, acc, parts, rows, points, leaf_of, col_of):
+def halo_kernel(near, counts, before, after, y_in, p_in, y_ref, g_ref, top_ref, acc, parts, rows, points, leaf_of, col_of):
     leaves = counts.shape[0]
     n_edge = HALO * 256
     for side, src in ((0, before), (1, after)):
@@ -160,6 +174,7 @@
             g_ref[at + n + c] = g_ref[at + 2 * c] + g_ref[at + 2 * c + 1]
         at += n
         n //= 2
+    packed(g_ref[at], top_ref)
 
 def edge_blocks(points, order, samples):
     n = HALO * 256
@@ -176,7 +191,7 @@
         2, (near, counts, points, order, samples))
 def halo_samples(near, counts, before, after, y, p):
     L = counts.shape[0]
-    return call(halo_kernel, [(L,256,128),(2*L-1,128,128)],
+    return call(halo_kernel, [(L,256,128),(2*L-1,128,128),(80,128)],
         [pltpu.VMEM((L+1,256,128),F32), pltpu.VMEM((2*HALO,256,256),BF16), pltpu.VMEM((L,3,256,128),F32), pltpu.VMEM((2*HALO,8,256),F32), pltpu.SMEM((64,),jnp.int32), pltpu.SMEM((64,),jnp.int32)],
         2, (near, counts, before, after, y, p))
 
@@ -195,14 +210,15 @@
     return jnp.broadcast_to(x[j : j + 1, :], x.shape)
 
 
-def factor_all(work, upper_out, inverse_out, groups):
+def factor_blocks(work, upper_out, inverse_out, groups, first=0, last=128 // BLK):
+    base = BLK * first
     lane = lax.broadcasted_iota(jnp.int32, (BLK, 128), 1)
     sub = lax.broadcasted_iota(jnp.int32, (BLK, 128), 0)
-    for k in range(128 // BLK):
+    for k in range(first, last):
         r = BLK * k
         on_diag = (lane >= r) & (lane < r + BLK)
         for group in groups:
-            panel = {m: work[m, r : r + BLK, :] for m in group}
+            panel = {m: work[m, r - base : r + BLK - base, :] for m in group}
             diag = None
             for s, m in enumerate(group):
                 shift = (BLK * s - r) % 128
@@ -222,23 +238,25 @@
                 scale = jnp.where(sub == j, rs, scale)
             inv = [e * scale for e in inv]
             for s, m in enumerate(group):
-                out = block = None
+                block, terms = None, []
                 for q in range(BLK):
                     x = jnp.broadcast_to(inv[q][:, BLK * s : BLK * s + 1], (BLK, 128))
-                    t = x * row_of(panel[m], q)
-                    out = t if q == 0 else out + t
+                    terms.append(x * row_of(panel[m], q))
                     block = x if q == 0 else jnp.where(lane == r + q, x, block)
-                upper_out[m, r : r + BLK, :] = jnp.where(lane >= r + sub, out, 0.0)
+                while len(terms) > 1:
+                    terms = [terms[t] + terms[t + 1] for t in range(0, len(terms), 2)]
+                out = terms[0]
+                upper_out[m, r - base : r + BLK - base, :] = jnp.where(lane >= r + sub, out, 0.0)
                 right = jnp.where(on_diag, block, out)
-                inverse_out[m, r : r + BLK, :] = jnp.where(lane < r + BLK, right, 0.0)
+                inverse_out[m, r - base : r + BLK - base, :] = jnp.where(lane < r + BLK, right, 0.0)
                 if r + BLK < 128:
                     p1, p2, p3 = pieces(right)
                     rhs = jnp.concatenate([p1, p2, p1, p2, p3, p1], axis=0).astype(BF16)
                     lhs = jnp.concatenate([p1, p1, p2, p2, p1, p3], axis=0).astype(BF16)
                     update = jnp.dot(lhs.T[r + BLK :], rhs, preferred_element_type=F32)
                     at = lax.broadcasted_iota(jnp.int32, (128 - r - BLK, 128), 1)
-                    old = work[m, r + BLK :, :]
-                    work[m, r + BLK :, :] = jnp.where((at >= r) & (at < r + BLK), 0.0, old) - update
+                    old = work[m, r + BLK - base :, :]
+                    work[m, r + BLK - base :, :] = jnp.where((at >= r) & (at < r + BLK), 0.0, old) - update
 
 
 def times_transposed(x, y):
@@ -247,20 +265,37 @@
     )
 
 
-def local_factor_kernel(g_ref, upper_ref, inverse_ref, work):
+def local_factor_kernel(first, last, g_ref, *refs):
+    *left, upper_ref, inverse_ref, work = refs
     work[...] = g_ref[...]
-    factor_all(work, upper_ref, inverse_ref, [list(range(g_ref.shape[0]))])
-
-
-def local_basis_kernel(y_ref, upper_ref, inverse_ref, leaf_ref, base_ref):
+    factor_blocks(work, upper_ref, inverse_ref, [list(range(g_ref.shape[0]))], first, last)
+    for out in left:
+        out[...] = work[:, BLK * (last - first) :, :]
+
+
+def local_factors(work, first, last):
+    n, rows, _ = work.shape
+    done = BLK * (last - first)
+    outs = [(n, rows - done, 128)] * (done < rows) + [(n, done, 128)] * 2
+    kernel = lambda *refs: local_factor_kernel(first, last, *refs)
+    return call(kernel, outs, [pltpu.VMEM(work.shape, F32)], 0, (work,))
+
+
+def whole(parts, m):
+    return jnp.concatenate([p[m] for p in parts], axis=0)
+
+
+def local_basis_kernel(y_ref, *refs):
+    *parts, leaf_ref, base_ref, root_ref = refs
+    upper, inverse = parts[: len(parts) // 2], parts[len(parts) // 2 :]
     leaves = y_ref.shape[0]
     for m in range(leaves):
-        leaf_ref[m * 256 : m * 256 + 256, :] = times_transposed(y_ref[m], inverse_ref[m])
+        leaf_ref[m * 256 : m * 256 + 256, :] = times_transposed(y_ref[m], whole(inverse, m))
     for n in range(leaves - 1):
+        inner = whole(inverse, leaves + n)
         for half in range(2):
-            base_ref[n, half * 128 : half * 128 + 128, :] = times_transposed(
-                upper_ref[2 * n + half], inverse_ref[leaves + n]
-            )
+            base_ref[n, half * 128 : half * 128 + 128, :] = times_transposed(whole(upper, 2 * n + half), inner)
+    root_ref[...] = whole(upper, 2 * leaves - 2)
 
 
 def upper_kernel(low_bits, *refs):
@@ -271,9 +306,9 @@
     base_ref, root_ref, work, upper, inverse = refs[1 + 2 * levels :]
     place = (lax.axis_index("tx") << low_bits) + lax.axis_index("ty")
     for m in range(levels):
-        work[m] = own[m][...]
-        work[levels + m] = partner[m][...]
-    factor_all(work, upper, inverse, [list(range(levels)), list(range(levels, 2 * levels))])
+        unpacked(own[m], work, m)
+        unpacked(partner[m], work, levels + m)
+    factor_blocks(work, upper, inverse, [list(range(levels)), list(range(levels, 2 * levels))])
     for h in range(levels):
         mine = first[...] if h == 0 else upper[h - 1]
         a = times_transposed(mine, inverse[h])
@@ -286,39 +321,41 @@
 
 def per_device(points, tree_order, samples, near_leaves, near_counts):
     leaves = near_counts.shape[0]
-    nodes = 2 * leaves - 1
     both = ("tx", "ty")
     for_after, for_before = edge_blocks(points, tree_order, samples)
     before = passed_along(for_after, both, 1)
     after = passed_along(for_before, both, -1)
     part, ordered = own_samples(near_leaves, near_counts, points, tree_order, samples)
-    sampled, grams = halo_samples(near_leaves, near_counts, before, after, part, ordered)
-    gram = grams[nodes - 1]
+    sampled, work, gram = halo_samples(near_leaves, near_counts, before, after, part, ordered)
     owns, partners = [], []
     low_bits = lax.axis_size("ty").bit_length() - 1
     high_bits = lax.axis_size("tx").bit_length() - 1
     steps = [("ty", m) for m in [1, 2, 4, 15]] + [("tx", m) for m in [1, 2, 6, 8, 24]]
     assert [m.bit_length() for _, m in steps] == [*range(1, low_bits + 1), *range(1, high_bits + 1)]
+    cuts = [0, 3, 8, 16]
+    uppers, inverses = [], []
     for h, (axis, mask) in enumerate(steps):
-        if h == 2:
-            grams, gram = lax.optimization_barrier((grams, gram))
+        factoring = h + 1 < len(cuts)
+        if factoring:
+            work, gram = lax.optimization_barrier((work, gram))
         if h == 3:
             sampled, gram = lax.optimization_barrier((sampled, gram))
         partner = exchanged(gram, axis, mask)
-        if h == 2:
-            uppers, inverses = call(
-                local_factor_kernel, [(nodes, 128, 128)] * 2, [pltpu.VMEM((nodes, 128, 128), F32)], 0, (grams,)
-            )
-            partner, uppers, inverses = lax.optimization_barrier((partner, uppers, inverses))
+        if factoring:
+            out = local_factors(work, cuts[h], cuts[h + 1])
+            partner, *out = lax.optimization_barrier((partner, *out))
+            work, upper, inverse = out if len(out) == 3 else (None, *out)
+            uppers.append(upper)
+            inverses.append(inverse)
         if h == 3:
-            leaf_bases, local_bases = call(
+            locals_out = call(
                 local_basis_kernel,
-                [(leaves * 256, 128), (leaves - 1, 256, 128)],
+                [(leaves * 256, 128), (leaves - 1, 256, 128), (128, 128)],
                 [],
                 0,
-                (sampled, uppers, inverses),
+                (sampled, *uppers, *inverses),
             )
-            partner, leaf_bases, local_bases = lax.optimization_barrier((partner, leaf_bases, local_bases))
+            partner, leaf_bases, local_bases, local_root = lax.optimization_barrier((partner, *locals_out))
         gram = gram + partner
         owns.append(gram)
         partners.append(partner)
@@ -328,7 +365,7 @@
         [(levels, 256, 128), (128, 128)],
         [pltpu.VMEM((2 * levels, 128, 128), F32)] * 3,
         0,
-        (uppers[nodes - 1], *owns, *partners),
+        (local_root, *owns, *partners),
     )
     return leaf_bases, local_bases, upper_bases, root
 

time: 129 us -> 123 us (0.953)
  waiting for transfers between devices: 28.4 us -> 17.7 us
  starting transfers between devices: 39 us -> 42.7 us
  Pallas kernels: 54.9 us -> 58.3 us
  local copies, waits for them, and re-layouts: 3.15 us -> 0.86 us
    ppermute x9, waiting for transfers between devices: 28.4 us -> 17.6 us  [exchanged(): lax.ppermute(value, axis, [(i, i ^ mask) for i in range(lax.axis_size(axi...]
    ppermute x9, starting transfers between devices: 23.9 us -> 27.6 us  [exchanged(): lax.ppermute(value, axis, [(i, i ^ mask) for i in range(lax.axis_size(axi...]
    pallas_call x5 -> x7, Pallas kernels: 53 us -> 56.4 us  [call(): pl.pallas_call(kernel, out_shape=tuple((jax.ShapeDtypeStruct(s, F32) for...]
    squeeze x2 -> x0, local copies, waits for them, and re-layouts: 2.3 us -> none  [the longest x1 1.46 us: per_device(): uppers[nodes - 1]]
  transfers between devices with their start and end apart: 11 -> 11, of which waited for: 7 -> 5; matrix products, arithmetic and copies ran while one was open for 1% -> 0% of each run, Pallas kernels for 23% -> 27%
where the time goes in v3:
time: 123 us; the launch traced here: 122 us
  Pallas kernels  58.3 us (47%)
  starting transfers between devices  42.7 us (35%)
  waiting for transfers between devices  17.7 us (14%)
  other arithmetic  1.49 us (1%)
    pallas_call x7, Pallas kernels, call(): pl.pallas_call(kernel, out_shape=tuple((jax.ShapeDtypeStruct(s, F32) for...  56.4 us
    ppermute x9, starting transfers between devices, exchanged(): lax.ppermute(value, axis, [(i, i ^ mask) for i in range(lax.axis_size(axi...  27.6 us
    ppermute x9, waiting for transfers between devices, exchanged(): lax.ppermute(value, axis, [(i, i ^ mask) for i in range(lax.axis_size(axi...  17.6 us
    ppermute x2, starting transfers between devices, passed_along(): return lax.ppermute(block, axis, route)  15.1 us
  transfers between devices with their start and end apart: 11, of which 5 were waited for; matrix products, arithmetic and copies ran while one was open for 0% of the time, Pallas kernels for 27%

profile of v3, /device:TPU:24, one launch (start us, length us, event | category | flops | bytes accessed | tf_op | source)
XLA Modules:
  0.0 121.9 jit_solution(12803404566827319284)
XLA Ops:
  0.6 1.9 %shard_map.84 = (f32[576,128]{1,0:T(8,128)}, f32[576,128]{1,0:T(8,128)}) custom-call(f32[2048,128]{1,0:T(8,128)} %own.1, f32[2048,128]{1,0:T(8,128)} %own.1, f32[3,2048]{1,0:T(4,128)} %raw.1, s32[1,2048]{1,0:T(1,128)} %order.3), custom_call_target="tpu_custom_call" | custom-call | tf_op jit(solution)/shard_map/pallas_call | solution.py:185
  2.5 3.8 %collective-permute-start = (f32[576,128]{1,0:T(8,128)}, f32[576,128]{1,0:T(8,128)S(1)}, u32[]{:S(2)}, u32[]{:S(2)}) collective-permute-start(f32[576,128]{1,0:T(8,128)} %get-tuple-element.47), channel_id=1, source_target_pairs={{0,1},{1,2},{2,3},{3,4},{4,5},{5,6},{6,7},{7,8},{8,9},{9,10},{10,1... | collective-permute-start | bytes 884744 | tf_op jit(solution)/shard_map/ppermute | solution.py:202
  6.3 11.3 %collective-permute-start.1 = (f32[576,128]{1,0:T(8,128)}, f32[576,128]{1,0:T(8,128)S(1)}, u32[]{:S(2)}, u32[]{:S(2)}) collective-permute-start(f32[576,128]{1,0:T(8,128)} %get-tuple-element.48), channel_id=1, source_target_pairs={{1,0},{2,1},{3,2},{4,3},{5,4},{6,5},{7,6},{8,7},{9,8},{10,9},{11,1... | collective-permute-start | bytes 884744 | tf_op jit(solution)/shard_map/ppermute | solution.py:202
  17.7 9.1 %shard_map.85 = (f32[8,256,128]{2,1,0:T(8,128)}, f32[8,8,256]{2,1,0:T(8,128)}) custom-call(s32[8,5]{1,0:T(8,128)} %near.3, s32[8]{0:T(128)} %counts.3, f32[3,2048]{1,0:T(4,128)} %raw.1, s32[1,2048]{1,0:T(1,128)} %order.3, f32[2048,128]{1,0:T(8,128)} %own.1), custom_call_target="tpu_custom_call" | custom-call | tf_op jit(solution)/shard_map/pallas_call | solution.py:23
  26.8 0.0 collective-permute-done.before
  26.8 0.0 collective-permute-done.1.after
  26.8 0.0 copy-start.9
  26.8 0.7 copy-done.8
  27.5 0.1 copy-done.9
  27.6 7.3 %shard_map.86 = (f32[8,256,128]{2,1,0:T(8,128)}, f32[15,128,128]{2,1,0:T(8,128)}, f32[80,128]{1,0:T(8,128)}) custom-call(s32[8,5]{1,0:T(8,128)} %near.3, s32[8]{0:T(128)} %counts.3, f32[576,128]{1,0:T(8,128)} %copy-done.8, f32[576,128]{1,0:T(8,128)} %copy-done.9, f32[8,256,128]{2,1,0:T(8,128)} %get-tuple-element.49.y_in, f32[8,8,256]{2,1,0:T(8,128)} %get-tuple-element.50.p_in), custom_call_target="tpu_custom_call" | custom-call | tf_op jit(solution)/shard_map/pallas_call | solution.py:23
  34.9 1.9 %collective-permute-start.2 = (f32[80,128]{1,0:T(8,128)}, f32[80,128]{1,0:T(8,128)S(1)}, u32[]{:S(2)}, u32[]{:S(2)}) collective-permute-start(f32[80,128]{1,0:T(8,128)} %get-tuple-element.54), channel_id=1, source_target_pairs={{0,1},{1,0},{2,3},{3,2},{4,5},{5,4},{6,7},{7,6},{8,9},{9,8},{10,11... | collective-permute-start | bytes 122888 | tf_op jit(solution)/shard_map/ppermute | solution.py:206
  36.8 4.5 %shard_map.87 = (f32[15,104,128]{2,1,0:T(8,128)}, f32[15,24,128]{2,1,0:T(8,128)}, f32[15,24,128]{2,1,0:T(8,128)}) custom-call(f32[15,128,128]{2,1,0:T(8,128)} %get-tuple-element.55.refs_0_), custom_call_target="tpu_custom_call" | custom-call | tf_op jit(solution)/shard_map/pallas_call | solution.py:23
  41.3 0.0 collective-permute-done.2.refs_10_
  41.3 0.8 add.27.refs_1_
  42.1 1.9 %collective-permute-start.3 = (f32[80,128]{1,0:T(8,128)S(1)}, f32[80,128]{1,0:T(8,128)S(1)}, u32[]{:S(2)}, u32[]{:S(2)}) collective-permute-start(f32[80,128]{1,0:T(8,128)S(1)} %add.27.refs_1_), channel_id=1, source_target_pairs={{0,2},{1,3},{2,0},{3,1},{4,6},{5,7},{6,4},{7,5},{8,10},{9,11},{10,... | collective-permute-start | bytes 122888 | tf_op jit(solution)/shard_map/ppermute | solution.py:206
  44.0 5.9 %shard_map.88 = (f32[15,64,128]{2,1,0:T(8,128)}, f32[15,40,128]{2,1,0:T(8,128)}, f32[15,40,128]{2,1,0:T(8,128)}) custom-call(f32[15,104,128]{2,1,0:T(8,128)} %get-tuple-element.62.refs_0_), custom_call_target="tpu_custom_call" | custom-call | tf_op jit(solution)/shard_map/pallas_call | solution.py:23
  49.9 0.0 collective-permute-done.3.refs_11_
  49.9 0.0 copy-start.1
  49.9 7.7 %collective-permute-start.4 = (f32[80,128]{1,0:T(8,128)S(1)}, f32[80,128]{1,0:T(8,128)S(1)}, u32[]{:S(2)}, u32[]{:S(2)}) collective-permute-start(f32[80,128]{1,0:T(8,128)S(1)} %add.28.refs_2_), channel_id=1, source_target_pairs={{0,4},{1,5},{2,6},{3,7},{4,0},{5,1},{6,2},{7,3},{8,12},{9,13},{10,... | collective-permute-start | bytes 122888 | tf_op jit(solution)/shard_map/ppermute | solution.py:206
  57.6 7.6 %shard_map.89 = (f32[15,64,128]{2,1,0:T(8,128)}, f32[15,64,128]{2,1,0:T(8,128)}) custom-call(f32[15,64,128]{2,1,0:T(8,128)} %get-tuple-element.69.refs_0_), custom_call_target="tpu_custom_call" | custom-call | tf_op jit(solution)/shard_map/pallas_call | solution.py:23
  65.3 0.0 collective-permute-done.4.refs_12_
  65.3 0.0 copy-start.2
  65.3 4.6 %collective-permute-start.5 = (f32[80,128]{1,0:T(8,128)S(1)}, f32[80,128]{1,0:T(8,128)S(1)}, u32[]{:S(2)}, u32[]{:S(2)}) collective-permute-start(f32[80,128]{1,0:T(8,128)S(1)} %add.29.refs_3_), channel_id=1, source_target_pairs={{0,15},{1,14},{2,13},{3,12},{4,11},{5,10},{6,9},{7,8},{8,7},{9,6},... | collective-permute-start | bytes 122888 | tf_op jit(solution)/shard_map/ppermute | solution.py:206
  69.9 5.6 %shard_map.90 = (f32[2048,128]{1,0:T(8,128)}, f32[7,256,128]{2,1,0:T(8,128)}, f32[128,128]{1,0:T(8,128)}) custom-call(f32[8,256,128]{2,1,0:T(8,128)} %get-tuple-element.74.y_ref, f32[15,24,128]{2,1,0:T(8,128)} %get-tuple-element.75.refs_0_, f32[15,40,128]{2,1,0:T(8,128)} %get-tuple-element.76.refs_1_, f32[15,64,128]{2,1,0:T(8,128)} %get-tuple-element.77.refs_2_, ...), custom_call_target="tpu_custom_call" | custom-call | tf_op jit(solution)/shard_map/pallas_call | solution.py:23
  75.5 0.0 copy-done.10
  75.5 0.0 copy-done
  75.5 0.0 copy-done.11
  75.5 0.0 copy-done.1
  75.5 0.0 copy-done.12
  75.5 0.0 collective-permute-done.5.refs_13_
  75.6 0.0 copy-start.13
  75.6 0.0 copy-done.2
  75.6 0.0 copy-start.3
  75.6 1.9 %collective-permute-start.6 = (f32[80,128]{1,0:T(8,128)S(1)}, f32[80,128]{1,0:T(8,128)S(1)}, u32[]{:S(2)}, u32[]{:S(2)}) collective-permute-start(f32[80,128]{1,0:T(8,128)S(1)} %add.30.refs_4_), channel_id=1, source_target_pairs={{0,16},{16,0},{32,48},{48,32},{64,80},{80,64},{96,112},{112,96},{1... | collective-permute-start | bytes 122888 | tf_op jit(solution)/shard_map/ppermute | solution.py:206
  77.5 1.2 collective-permute-done.6.refs_14_
  78.7 0.0 copy-start.4
  78.7 1.9 %collective-permute-start.7 = (f32[80,128]{1,0:T(8,128)S(1)}, f32[80,128]{1,0:T(8,128)S(1)}, u32[]{:S(2)}, u32[]{:S(2)}) collective-permute-start(f32[80,128]{1,0:T(8,128)S(1)} %add.31.refs_5_), channel_id=1, source_target_pairs={{0,32},{16,48},{32,0},{48,16},{64,96},{80,112},{96,64},{112,80},{1... | collective-permute-start | bytes 122888 | tf_op jit(solution)/shard_map/ppermute | solution.py:206
  80.7 4.0 %collective-permute-done.7.refs_15_ = f32[80,128]{1,0:T(8,128)S(1)} collective-permute-done((f32[80,128]{1,0:T(8,128)S(1)}, f32[80,128]{1,0:T(8,128)S(1)}, u32[]{:S(2)}, u32[]{:S(2)}) %collective-permute-start.7) | collective-permute-done | bytes 40992 | tf_op jit(solution)/shard_map/ppermute | solution.py:206
  84.6 0.0 copy-start.5
  84.7 3.2 %collective-permute-start.8 = (f32[80,128]{1,0:T(8,128)S(1)}, f32[80,128]{1,0:T(8,128)S(1)}, u32[]{:S(2)}, u32[]{:S(2)}) collective-permute-start(f32[80,128]{1,0:T(8,128)S(1)} %add.32.refs_6_), channel_id=1, source_target_pairs={{0,96},{16,112},{32,64},{48,80},{64,32},{80,48},{96,0},{112,16},{1... | collective-permute-start | bytes 122888 | tf_op jit(solution)/shard_map/ppermute | solution.py:206
  87.9 3.9 %collective-permute-done.8.refs_16_ = f32[80,128]{1,0:T(8,128)S(1)} collective-permute-done((f32[80,128]{1,0:T(8,128)S(1)}, f32[80,128]{1,0:T(8,128)S(1)}, u32[]{:S(2)}, u32[]{:S(2)}) %collective-permute-start.8) | collective-permute-done | bytes 40992 | tf_op jit(solution)/shard_map/ppermute | solution.py:206
  91.8 2.3 %collective-permute-start.9 = (f32[80,128]{1,0:T(8,128)S(1)}, f32[80,128]{1,0:T(8,128)S(1)}, u32[]{:S(2)}, u32[]{:S(2)}) collective-permute-start(f32[80,128]{1,0:T(8,128)S(1)} %add.33.refs_7_), channel_id=1, source_target_pairs={{0,128},{16,144},{32,160},{48,176},{64,192},{80,208},{96,224},{112... | collective-permute-start | bytes 122888 | tf_op jit(solution)/shard_map/ppermute | solution.py:206
  94.1 3.6 %collective-permute-done.9.refs_17_ = f32[80,128]{1,0:T(8,128)S(1)} collective-permute-done((f32[80,128]{1,0:T(8,128)S(1)}, f32[80,128]{1,0:T(8,128)S(1)}, u32[]{:S(2)}, u32[]{:S(2)}) %collective-permute-start.9) | collective-permute-done | bytes 40992 | tf_op jit(solution)/shard_map/ppermute | solution.py:206
  97.7 2.1 %collective-permute-start.10 = (f32[80,128]{1,0:T(8,128)S(1)}, f32[80,128]{1,0:T(8,128)S(1)}, u32[]{:S(2)}, u32[]{:S(2)}) collective-permute-start(f32[80,128]{1,0:T(8,128)S(1)} %add.34.refs_8_), channel_id=1, source_target_pairs={{0,384},{16,400},{32,416},{48,432},{64,448},{80,464},{96,480},{112... | collective-permute-start | bytes 122888 | tf_op jit(solution)/shard_map/ppermute | solution.py:206
  99.8 5.0 %collective-permute-done.10.refs_18_ = f32[80,128]{1,0:T(8,128)S(1)} collective-permute-done((f32[80,128]{1,0:T(8,128)S(1)}, f32[80,128]{1,0:T(8,128)S(1)}, u32[]{:S(2)}, u32[]{:S(2)}) %collective-permute-start.10) | collective-permute-done | bytes 40992 | tf_op jit(solution)/shard_map/ppermute | solution.py:206
  104.8 0.6 add.35.refs_9_
  105.5 0.0 copy-done.14
  105.5 16.4 %shard_map.91 = (f32[9,256,128]{2,1,0:T(8,128)}, f32[128,128]{1,0:T(8,128)}) custom-call(f32[128,128]{1,0:T(8,128)} %get-tuple-element.86.refs_0_, f32[80,128]{1,0:T(8,128)} %copy-done, f32[80,128]{1,0:T(8,128)} %copy-done.1, f32[80,128]{1,0:T(8,128)} %copy-done.2, f32[80,128]{1,0:T(8,128)} %copy-done.3, f32[80,128]{1,0:T(8,128)} %copy-done.4, ...), custom_call_target="tpu_custom_call" | custom-call | tf_op jit(solution)/shard_map/pallas_call | solution.py:23
  (29 shorter events, 0.1 us)
Async XLA Ops:
  2.5 24.3 %collective-permute-start = (f32[576,128]{1,0:T(8,128)}, f32[576,128]{1,0:T(8,128)S(1)}, u32[]{:S(2)}, u32[]{:S(2)}) collective-permute-start(f32[576,128]{1,0:T(8,128)} %get-tuple-element.47), channel_id=1, source_target_pairs={{0,1},{1,2},{2,3},{3,4},{4,5},{5,6},{6,7},{7,8},{8,9},{9,10},{10,1... | collective-permute-start | bytes 884744 | tf_op jit(solution)/shard_map/ppermute | solution.py:202
  6.3 20.5 %collective-permute-start.1 = (f32[576,128]{1,0:T(8,128)}, f32[576,128]{1,0:T(8,128)S(1)}, u32[]{:S(2)}, u32[]{:S(2)}) collective-permute-start(f32[576,128]{1,0:T(8,128)} %get-tuple-element.48), channel_id=1, source_target_pairs={{1,0},{2,1},{3,2},{4,3},{5,4},{6,5},{7,6},{8,7},{9,8},{10,9},{11,1... | collective-permute-start | bytes 884744 | tf_op jit(solution)/shard_map/ppermute | solution.py:202
  26.8 0.7 copy-start.8
  26.8 0.8 copy-start.9
  34.9 6.4 %collective-permute-start.2 = (f32[80,128]{1,0:T(8,128)}, f32[80,128]{1,0:T(8,128)S(1)}, u32[]{:S(2)}, u32[]{:S(2)}) collective-permute-start(f32[80,128]{1,0:T(8,128)} %get-tuple-element.54), channel_id=1, source_target_pairs={{0,1},{1,0},{2,3},{3,2},{4,5},{5,4},{6,7},{7,6},{8,9},{9,8},{10,11... | collective-permute-start | bytes 122888 | tf_op jit(solution)/shard_map/ppermute | solution.py:206
  41.3 34.2 %copy-start.10 = (f32[80,128]{1,0:T(8,128)}, f32[80,128]{1,0:T(8,128)S(1)}, u32[]{:S(2)}) copy-start(f32[80,128]{1,0:T(8,128)S(1)} %collective-permute-done.2.refs_10_) | copy-start | bytes 122884
  42.1 33.4 %copy-start = (f32[80,128]{1,0:T(8,128)}, f32[80,128]{1,0:T(8,128)S(1)}, u32[]{:S(2)}) copy-start(f32[80,128]{1,0:T(8,128)S(1)} %add.27.refs_1_) | copy-start | bytes 122884
  42.1 7.8 %collective-permute-start.3 = (f32[80,128]{1,0:T(8,128)S(1)}, f32[80,128]{1,0:T(8,128)S(1)}, u32[]{:S(2)}, u32[]{:S(2)}) collective-permute-start(f32[80,128]{1,0:T(8,128)S(1)} %add.27.refs_1_), channel_id=1, source_target_pairs={{0,2},{1,3},{2,0},{3,1},{4,6},{5,7},{6,4},{7,5},{8,10},{9,11},{10,... | collective-permute-start | bytes 122888 | tf_op jit(solution)/shard_map/ppermute | solution.py:206
  49.9 25.6 %copy-start.11 = (f32[80,128]{1,0:T(8,128)}, f32[80,128]{1,0:T(8,128)S(1)}, u32[]{:S(2)}) copy-start(f32[80,128]{1,0:T(8,128)S(1)} %collective-permute-done.3.refs_11_) | copy-start | bytes 122884
  49.9 25.6 %copy-start.1 = (f32[80,128]{1,0:T(8,128)}, f32[80,128]{1,0:T(8,128)S(1)}, u32[]{:S(2)}) copy-start(f32[80,128]{1,0:T(8,128)S(1)} %add.28.refs_2_) | copy-start | bytes 122884
  49.9 15.4 %collective-permute-start.4 = (f32[80,128]{1,0:T(8,128)S(1)}, f32[80,128]{1,0:T(8,128)S(1)}, u32[]{:S(2)}, u32[]{:S(2)}) collective-permute-start(f32[80,128]{1,0:T(8,128)S(1)} %add.28.refs_2_), channel_id=1, source_target_pairs={{0,4},{1,5},{2,6},{3,7},{4,0},{5,1},{6,2},{7,3},{8,12},{9,13},{10,... | collective-permute-start | bytes 122888 | tf_op jit(solution)/shard_map/ppermute | solution.py:206
  65.3 10.3 %copy-start.12 = (f32[80,128]{1,0:T(8,128)}, f32[80,128]{1,0:T(8,128)S(1)}, u32[]{:S(2)}) copy-start(f32[80,128]{1,0:T(8,128)S(1)} %collective-permute-done.4.refs_12_) | copy-start | bytes 122884
  65.3 10.3 %copy-start.2 = (f32[80,128]{1,0:T(8,128)}, f32[80,128]{1,0:T(8,128)S(1)}, u32[]{:S(2)}) copy-start(f32[80,128]{1,0:T(8,128)S(1)} %add.29.refs_3_) | copy-start | bytes 122884
  65.3 10.3 %collective-permute-start.5 = (f32[80,128]{1,0:T(8,128)S(1)}, f32[80,128]{1,0:T(8,128)S(1)}, u32[]{:S(2)}, u32[]{:S(2)}) collective-permute-start(f32[80,128]{1,0:T(8,128)S(1)} %add.29.refs_3_), channel_id=1, source_target_pairs={{0,15},{1,14},{2,13},{3,12},{4,11},{5,10},{6,9},{7,8},{8,7},{9,6},... | collective-permute-start | bytes 122888 | tf_op jit(solution)/shard_map/ppermute | solution.py:206
  75.6 29.9 %copy-start.13 = (f32[80,128]{1,0:T(8,128)}, f32[80,128]{1,0:T(8,128)S(1)}, u32[]{:S(2)}) copy-start(f32[80,128]{1,0:T(8,128)S(1)} %collective-permute-done.5.refs_13_) | copy-start | bytes 122884
  75.6 29.9 %copy-start.3 = (f32[80,128]{1,0:T(8,128)}, f32[80,128]{1,0:T(8,128)S(1)}, u32[]{:S(2)}) copy-start(f32[80,128]{1,0:T(8,128)S(1)} %add.30.refs_4_) | copy-start | bytes 122884
  75.6 3.1 %collective-permute-start.6 = (f32[80,128]{1,0:T(8,128)S(1)}, f32[80,128]{1,0:T(8,128)S(1)}, u32[]{:S(2)}, u32[]{:S(2)}) collective-permute-start(f32[80,128]{1,0:T(8,128)S(1)} %add.30.refs_4_), channel_id=1, source_target_pairs={{0,16},{16,0},{32,48},{48,32},{64,80},{80,64},{96,112},{112,96},{1... | collective-permute-start | bytes 122888 | tf_op jit(solution)/shard_map/ppermute | solution.py:206
  78.7 26.7 %copy-start.14 = (f32[80,128]{1,0:T(8,128)}, f32[80,128]{1,0:T(8,128)S(1)}, u32[]{:S(2)}) copy-start(f32[80,128]{1,0:T(8,128)S(1)} %collective-permute-done.6.refs_14_) | copy-start | bytes 122884
  78.7 26.7 %copy-start.4 = (f32[80,128]{1,0:T(8,128)}, f32[80,128]{1,0:T(8,128)S(1)}, u32[]{:S(2)}) copy-start(f32[80,128]{1,0:T(8,128)S(1)} %add.31.refs_5_) | copy-start | bytes 122884
  78.7 5.9 %collective-permute-start.7 = (f32[80,128]{1,0:T(8,128)S(1)}, f32[80,128]{1,0:T(8,128)S(1)}, u32[]{:S(2)}, u32[]{:S(2)}) collective-permute-start(f32[80,128]{1,0:T(8,128)S(1)} %add.31.refs_5_), channel_id=1, source_target_pairs={{0,32},{16,48},{32,0},{48,16},{64,96},{80,112},{96,64},{112,80},{1... | collective-permute-start | bytes 122888 | tf_op jit(solution)/shard_map/ppermute | solution.py:206
  84.6 20.8 %copy-start.15 = (f32[80,128]{1,0:T(8,128)}, f32[80,128]{1,0:T(8,128)S(1)}, u32[]{:S(2)}) copy-start(f32[80,128]{1,0:T(8,128)S(1)} %collective-permute-done.7.refs_15_) | copy-start | bytes 122884
  84.6 20.8 %copy-start.5 = (f32[80,128]{1,0:T(8,128)}, f32[80,128]{1,0:T(8,128)S(1)}, u32[]{:S(2)}) copy-start(f32[80,128]{1,0:T(8,128)S(1)} %add.32.refs_6_) | copy-start | bytes 122884
  84.7 7.1 %collective-permute-start.8 = (f32[80,128]{1,0:T(8,128)S(1)}, f32[80,128]{1,0:T(8,128)S(1)}, u32[]{:S(2)}, u32[]{:S(2)}) collective-permute-start(f32[80,128]{1,0:T(8,128)S(1)} %add.32.refs_6_), channel_id=1, source_target_pairs={{0,96},{16,112},{32,64},{48,80},{64,32},{80,48},{96,0},{112,16},{1... | collective-permute-start | bytes 122888 | tf_op jit(solution)/shard_map/ppermute | solution.py:206
  91.8 13.7 %copy-start.16 = (f32[80,128]{1,0:T(8,128)}, f32[80,128]{1,0:T(8,128)S(1)}, u32[]{:S(2)}) copy-start(f32[80,128]{1,0:T(8,128)S(1)} %collective-permute-done.8.refs_16_) | copy-start | bytes 122884
  91.8 13.7 %copy-start.6 = (f32[80,128]{1,0:T(8,128)}, f32[80,128]{1,0:T(8,128)S(1)}, u32[]{:S(2)}) copy-start(f32[80,128]{1,0:T(8,128)S(1)} %add.33.refs_7_) | copy-start | bytes 122884
  91.8 5.9 %collective-permute-start.9 = (f32[80,128]{1,0:T(8,128)S(1)}, f32[80,128]{1,0:T(8,128)S(1)}, u32[]{:S(2)}, u32[]{:S(2)}) collective-permute-start(f32[80,128]{1,0:T(8,128)S(1)} %add.33.refs_7_), channel_id=1, source_target_pairs={{0,128},{16,144},{32,160},{48,176},{64,192},{80,208},{96,224},{112... | collective-permute-start | bytes 122888 | tf_op jit(solution)/shard_map/ppermute | solution.py:206
  97.7 7.8 %copy-start.17 = (f32[80,128]{1,0:T(8,128)}, f32[80,128]{1,0:T(8,128)S(1)}, u32[]{:S(2)}) copy-start(f32[80,128]{1,0:T(8,128)S(1)} %collective-permute-done.9.refs_17_) | copy-start | bytes 122884
  97.7 7.8 %copy-start.7 = (f32[80,128]{1,0:T(8,128)}, f32[80,128]{1,0:T(8,128)S(1)}, u32[]{:S(2)}) copy-start(f32[80,128]{1,0:T(8,128)S(1)} %add.34.refs_8_) | copy-start | bytes 122884
  97.7 7.1 %collective-permute-start.10 = (f32[80,128]{1,0:T(8,128)S(1)}, f32[80,128]{1,0:T(8,128)S(1)}, u32[]{:S(2)}, u32[]{:S(2)}) collective-permute-start(f32[80,128]{1,0:T(8,128)S(1)} %add.34.refs_8_), channel_id=1, source_target_pairs={{0,384},{16,400},{32,416},{48,432},{64,448},{80,464},{96,480},{112... | collective-permute-start | bytes 122888 | tf_op jit(solution)/shard_map/ppermute | solution.py:206
  104.8 0.7 copy-start.18

commit v4 on v3

--- a/solution.py
+++ b/solution.py
@@ -298,25 +298,42 @@
     root_ref[...] = whole(upper, 2 * leaves - 2)
 
 
-def upper_kernel(low_bits, *refs):
-    levels = (len(refs) - 6) // 2
-    first = refs[0]
-    own = refs[1 : 1 + levels]
-    partner = refs[1 + levels : 1 + 2 * levels]
-    base_ref, root_ref, work, upper, inverse = refs[1 + 2 * levels :]
+def first_factor_kernel(last, *refs):
+    *packs, left, upper_ref, inverse_ref, work = refs
+    for m, p in enumerate(packs):
+        unpacked(p, work, m)
+    factor_blocks(work, upper_ref, inverse_ref, [list(range(len(packs)))], 0, last)
+    left[...] = work[:, BLK * last :, :]
+
+
+def first_factors(packs, last):
+    n, done = len(packs), BLK * last
+    outs = [(n, 128 - done, 128), (n, done, 128), (n, done, 128)]
+    kernel = lambda *refs: first_factor_kernel(last, *refs)
+    return call(kernel, outs, [pltpu.VMEM((n, 128, 128), F32)], 0, tuple(packs))
+
+
+def upper_kernel(low_bits, low, high, *refs):
+    first, refs = refs[0], refs[1:]
+    parts = (len(refs) - 2 * high - 5) // 2
+    low_upper, low_inverse = refs[:parts], refs[parts : 2 * parts]
+    packs = refs[2 * parts : 2 * parts + 2 * high]
+    base_ref, root_ref, work, upper, inverse = refs[2 * parts + 2 * high :]
     place = (lax.axis_index("tx") << low_bits) + lax.axis_index("ty")
-    for m in range(levels):
-        unpacked(own[m], work, m)
-        unpacked(partner[m], work, levels + m)
-    factor_blocks(work, upper, inverse, [list(range(levels)), list(range(levels, 2 * levels))])
-    for h in range(levels):
-        mine = first[...] if h == 0 else upper[h - 1]
-        a = times_transposed(mine, inverse[h])
-        b = times_transposed(upper[levels + h], inverse[h])
+    for m, p in enumerate(packs):
+        unpacked(p, work, m)
+    factor_blocks(work, upper, inverse, [list(range(2 * high))])
+    for h in range(low + high):
+        if h == 0:
+            mine = first[...]
+        else:
+            mine = whole(low_upper, h - 1) if h <= low else upper[h - 1 - low]
+        other = whole(low_upper, low + h) if h < low else upper[high + h - low]
+        inner = whole(low_inverse, h) if h < low else inverse[h - low]
         bit = (place >> h) & 1
-        base_ref[h, pl.ds(bit * 128, 128), :] = a
-        base_ref[h, pl.ds((1 - bit) * 128, 128), :] = b
-    root_ref[...] = upper[levels - 1]
+        base_ref[h, pl.ds(bit * 128, 128), :] = times_transposed(mine, inner)
+        base_ref[h, pl.ds((1 - bit) * 128, 128), :] = times_transposed(other, inner)
+    root_ref[...] = upper[high - 1]
 
 
 def per_device(points, tree_order, samples, near_leaves, near_counts):
@@ -333,13 +350,15 @@
     steps = [("ty", m) for m in [1, 2, 4, 15]] + [("tx", m) for m in [1, 2, 6, 8, 24]]
     assert [m.bit_length() for _, m in steps] == [*range(1, low_bits + 1), *range(1, high_bits + 1)]
     cuts = [0, 3, 8, 16]
-    uppers, inverses = [], []
+    uppers, inverses, low_uppers, low_inverses = [], [], [], []
     for h, (axis, mask) in enumerate(steps):
         factoring = h + 1 < len(cuts)
         if factoring:
             work, gram = lax.optimization_barrier((work, gram))
         if h == 3:
             sampled, gram = lax.optimization_barrier((sampled, gram))
+        if h > low_bits + 1:
+            low_work, gram = lax.optimization_barrier((low_work, gram))
         partner = exchanged(gram, axis, mask)
         if factoring:
             out = local_factors(work, cuts[h], cuts[h + 1])
@@ -356,16 +375,26 @@
                 (sampled, *uppers, *inverses),
             )
             partner, leaf_bases, local_bases, local_root = lax.optimization_barrier((partner, *locals_out))
+        if h >= low_bits + 1:
+            if h == low_bits + 1:
+                out = first_factors([*owns[:low_bits], *partners[:low_bits]], 4)
+            else:
+                out = local_factors(low_work, low_at, low_at + 4)
+            low_at = 4 if h == low_bits + 1 else low_at + 4
+            partner, *out = lax.optimization_barrier((partner, *out))
+            low_work, upper, inverse = out if len(out) == 3 else (None, *out)
+            low_uppers.append(upper)
+            low_inverses.append(inverse)
         gram = gram + partner
         owns.append(gram)
         partners.append(partner)
     levels = len(owns)
     upper_bases, root = call(
-        lambda *refs: upper_kernel(low_bits, *refs),
+        lambda *refs: upper_kernel(low_bits, low_bits, high_bits, *refs),
         [(levels, 256, 128), (128, 128)],
-        [pltpu.VMEM((2 * levels, 128, 128), F32)] * 3,
+        [pltpu.VMEM((2 * high_bits, 128, 128), F32)] * 3,
         0,
-        (local_root, *owns, *partners),
+        (local_root, *low_uppers, *low_inverses, *owns[low_bits:], *partners[low_bits:]),
     )
     return leaf_bases, local_bases, upper_bases, root
 

time: 123 us -> 125 us (1.016)
  the two profiles are of different devices: /device:TPU:24 before, /device:TPU:1 now
where the time goes in v4:
time: 125 us; the launch traced here: 124 us
  Pallas kernels  71.6 us (57%)
  starting transfers between devices  48.2 us (39%)
  other arithmetic  1.47 us (1%)
    pallas_call x11, Pallas kernels, call(): pl.pallas_call(kernel, out_shape=tuple((jax.ShapeDtypeStruct(s, F32) for...  69.7 us
    ppermute x9, starting transfers between devices, exchanged(): lax.ppermute(value, axis, [(i, i ^ mask) for i in range(lax.axis_size(axi...  33.8 us
    ppermute x2, starting transfers between devices, passed_along(): return lax.ppermute(block, axis, route)  14.4 us
  transfers between devices with their start and end apart: 11, of which 1 were waited for; matrix products, arithmetic and copies ran while one was open for 0% of the time, Pallas kernels for 39%

profile of v4, /device:TPU:1, one launch (start us, length us, event | category | flops | bytes accessed | tf_op | source)
XLA Modules:
  0.0 123.9 jit_solution(16917914081221484980)
XLA Ops:
  0.6 1.9 %shard_map.84 = (f32[576,128]{1,0:T(8,128)}, f32[576,128]{1,0:T(8,128)}) custom-call(f32[2048,128]{1,0:T(8,128)} %own.1, f32[2048,128]{1,0:T(8,128)} %own.1, f32[3,2048]{1,0:T(4,128)} %raw.1, s32[1,2048]{1,0:T(1,128)} %order.3), custom_call_target="tpu_custom_call" | custom-call | tf_op jit(solution)/shard_map/pallas_call | solution.py:185
  2.5 4.4 %collective-permute-start = (f32[576,128]{1,0:T(8,128)}, f32[576,128]{1,0:T(8,128)S(1)}, u32[]{:S(2)}, u32[]{:S(2)}) collective-permute-start(f32[576,128]{1,0:T(8,128)} %get-tuple-element.79), channel_id=1, source_target_pairs={{0,1},{1,2},{2,3},{3,4},{4,5},{5,6},{6,7},{7,8},{8,9},{9,10},{10,1... | collective-permute-start | bytes 884744 | tf_op jit(solution)/shard_map/ppermute | solution.py:202
  6.9 10.1 %collective-permute-start.1 = (f32[576,128]{1,0:T(8,128)}, f32[576,128]{1,0:T(8,128)S(1)}, u32[]{:S(2)}, u32[]{:S(2)}) collective-permute-start(f32[576,128]{1,0:T(8,128)} %get-tuple-element.80), channel_id=1, source_target_pairs={{1,0},{2,1},{3,2},{4,3},{5,4},{6,5},{7,6},{8,7},{9,8},{10,9},{11,1... | collective-permute-start | bytes 884744 | tf_op jit(solution)/shard_map/ppermute | solution.py:202
  17.0 9.1 %shard_map.85 = (f32[8,256,128]{2,1,0:T(8,128)}, f32[8,8,256]{2,1,0:T(8,128)}) custom-call(s32[8,5]{1,0:T(8,128)} %near.3, s32[8]{0:T(128)} %counts.3, f32[3,2048]{1,0:T(4,128)} %raw.1, s32[1,2048]{1,0:T(1,128)} %order.3, f32[2048,128]{1,0:T(8,128)} %own.1), custom_call_target="tpu_custom_call" | custom-call | tf_op jit(solution)/shard_map/pallas_call | solution.py:23
  26.1 0.0 collective-permute-done.before
  26.1 0.0 collective-permute-done.1.after
  26.1 0.0 copy-start.9
  26.1 0.7 copy-done.8
  26.8 0.1 copy-done.9
  26.9 7.2 %shard_map.86 = (f32[8,256,128]{2,1,0:T(8,128)}, f32[15,128,128]{2,1,0:T(8,128)}, f32[80,128]{1,0:T(8,128)}) custom-call(s32[8,5]{1,0:T(8,128)} %near.3, s32[8]{0:T(128)} %counts.3, f32[576,128]{1,0:T(8,128)} %copy-done.8, f32[576,128]{1,0:T(8,128)} %copy-done.9, f32[8,256,128]{2,1,0:T(8,128)} %get-tuple-element.81.y_in, f32[8,8,256]{2,1,0:T(8,128)} %get-tuple-element.82.p_in), custom_call_target="tpu_custom_call" | custom-call | tf_op jit(solution)/shard_map/pallas_call | solution.py:23
  34.1 1.9 %collective-permute-start.2 = (f32[80,128]{1,0:T(8,128)}, f32[80,128]{1,0:T(8,128)S(1)}, u32[]{:S(2)}, u32[]{:S(2)}) collective-permute-start(f32[80,128]{1,0:T(8,128)} %get-tuple-element.86), channel_id=1, source_target_pairs={{0,1},{1,0},{2,3},{3,2},{4,5},{5,4},{6,7},{7,6},{8,9},{9,8},{10,11... | collective-permute-start | bytes 122888 | tf_op jit(solution)/shard_map/ppermute | solution.py:206
  36.0 4.5 %shard_map.87 = (f32[15,104,128]{2,1,0:T(8,128)}, f32[15,24,128]{2,1,0:T(8,128)}, f32[15,24,128]{2,1,0:T(8,128)}) custom-call(f32[15,128,128]{2,1,0:T(8,128)} %get-tuple-element.87.refs_0_), custom_call_target="tpu_custom_call" | custom-call | tf_op jit(solution)/shard_map/pallas_call | solution.py:23
  40.5 0.0 collective-permute-done.2.refs_4_
  40.5 0.8 add.27.refs_0_
  41.3 1.9 %collective-permute-start.3 = (f32[80,128]{1,0:T(8,128)S(1)}, f32[80,128]{1,0:T(8,128)S(1)}, u32[]{:S(2)}, u32[]{:S(2)}) collective-permute-start(f32[80,128]{1,0:T(8,128)S(1)} %add.27.refs_0_), channel_id=1, source_target_pairs={{0,2},{1,3},{2,0},{3,1},{4,6},{5,7},{6,4},{7,5},{8,10},{9,11},{10,... | collective-permute-start | bytes 122888 | tf_op jit(solution)/shard_map/ppermute | solution.py:206
  43.3 5.9 %shard_map.88 = (f32[15,64,128]{2,1,0:T(8,128)}, f32[15,40,128]{2,1,0:T(8,128)}, f32[15,40,128]{2,1,0:T(8,128)}) custom-call(f32[15,104,128]{2,1,0:T(8,128)} %get-tuple-element.94.refs_0_), custom_call_target="tpu_custom_call" | custom-call | tf_op jit(solution)/shard_map/pallas_call | solution.py:23
  49.1 0.0 collective-permute-done.3.refs_5_
  49.1 0.0 copy-start.5
  49.2 6.2 %collective-permute-start.4 = (f32[80,128]{1,0:T(8,128)S(1)}, f32[80,128]{1,0:T(8,128)S(1)}, u32[]{:S(2)}, u32[]{:S(2)}) collective-permute-start(f32[80,128]{1,0:T(8,128)S(1)} %add.28.refs_1_), channel_id=1, source_target_pairs={{0,4},{1,5},{2,6},{3,7},{4,0},{5,1},{6,2},{7,3},{8,12},{9,13},{10,... | collective-permute-start | bytes 122888 | tf_op jit(solution)/shard_map/ppermute | solution.py:206
  55.3 7.6 %shard_map.89 = (f32[15,64,128]{2,1,0:T(8,128)}, f32[15,64,128]{2,1,0:T(8,128)}) custom-call(f32[15,64,128]{2,1,0:T(8,128)} %get-tuple-element.101.refs_0_), custom_call_target="tpu_custom_call" | custom-call | tf_op jit(solution)/shard_map/pallas_call | solution.py:23
  63.0 0.0 collective-permute-done.4.refs_6_
  63.0 0.0 copy-start.6
  63.0 6.5 %collective-permute-start.5 = (f32[80,128]{1,0:T(8,128)S(1)}, f32[80,128]{1,0:T(8,128)S(1)}, u32[]{:S(2)}, u32[]{:S(2)}) collective-permute-start(f32[80,128]{1,0:T(8,128)S(1)} %add.29.refs_2_), channel_id=1, source_target_pairs={{0,15},{1,14},{2,13},{3,12},{4,11},{5,10},{6,9},{7,8},{8,7},{9,6},... | collective-permute-start | bytes 122888 | tf_op jit(solution)/shard_map/ppermute | solution.py:206
  69.5 5.6 %shard_map.90 = (f32[2048,128]{1,0:T(8,128)}, f32[7,256,128]{2,1,0:T(8,128)}, f32[128,128]{1,0:T(8,128)}) custom-call(f32[8,256,128]{2,1,0:T(8,128)} %get-tuple-element.106.y_ref, f32[15,24,128]{2,1,0:T(8,128)} %get-tuple-element.107.refs_0_, f32[15,40,128]{2,1,0:T(8,128)} %get-tuple-element.108.refs_1_, f32[15,64,128]{2,1,0:T(8,128)} %get-tuple-element.109.refs_2_, ...), custom_call_target="tpu_custom_call" | custom-call | tf_op jit(solution)/shard_map/pallas_call | solution.py:23
  75.1 0.0 copy-done.15
  75.1 0.0 copy-done.4
  75.2 0.0 copy-done.16
  75.2 0.0 copy-done.5
  75.2 0.0 collective-permute-done.5.refs_7_
  75.2 0.0 copy-start.7
  75.2 5.7 %collective-permute-start.6 = (f32[80,128]{1,0:T(8,128)S(1)}, f32[80,128]{1,0:T(8,128)S(1)}, u32[]{:S(2)}, u32[]{:S(2)}) collective-permute-start(f32[80,128]{1,0:T(8,128)S(1)} %add.30.refs_3_), channel_id=1, source_target_pairs={{0,16},{16,0},{32,48},{48,32},{64,80},{80,64},{96,112},{112,96},{1... | collective-permute-start | bytes 122888 | tf_op jit(solution)/shard_map/ppermute | solution.py:206
  81.0 0.8 collective-permute-done.6.refs_14_
  81.8 1.9 %collective-permute-start.7 = (f32[80,128]{1,0:T(8,128)S(1)}, f32[80,128]{1,0:T(8,128)S(1)}, u32[]{:S(2)}, u32[]{:S(2)}) collective-permute-start(f32[80,128]{1,0:T(8,128)S(1)} %add.31.refs_9_), channel_id=1, source_target_pairs={{0,32},{16,48},{32,0},{48,16},{64,96},{80,112},{96,64},{112,80},{1... | collective-permute-start | bytes 122888 | tf_op jit(solution)/shard_map/ppermute | solution.py:206
  83.8 4.2 %shard_map.91 = (f32[8,96,128]{2,1,0:T(8,128)}, f32[8,32,128]{2,1,0:T(8,128)}, f32[8,32,128]{2,1,0:T(8,128)}) custom-call(f32[80,128]{1,0:T(8,128)} %copy-done.4, f32[80,128]{1,0:T(8,128)} %copy-done.5, f32[80,128]{1,0:T(8,128)} %copy-done.6, f32[80,128]{1,0:T(8,128)} %copy-done.7, f32[80,128]{1,0:T(8,128)} %copy-done.15, f32[80,128]{1,0:T(8,128)} %copy-done.16, ...), custom_call_target="tpu_custom_call" | custom-call | tf_op jit(solution)/shard_map/pallas_call | solution.py:23
  88.0 0.0 collective-permute-done.7.refs_15_
  88.0 2.9 %collective-permute-start.8 = (f32[80,128]{1,0:T(8,128)S(1)}, f32[80,128]{1,0:T(8,128)S(1)}, u32[]{:S(2)}, u32[]{:S(2)}) collective-permute-start(f32[80,128]{1,0:T(8,128)S(1)} %add.32.refs_10_), channel_id=1, source_target_pairs={{0,96},{16,112},{32,64},{48,80},{64,32},{80,48},{96,0},{112,16},{1... | collective-permute-start | bytes 122888 | tf_op jit(solution)/shard_map/ppermute | solution.py:206
  90.9 4.1 %shard_map.92 = (f32[8,64,128]{2,1,0:T(8,128)}, f32[8,32,128]{2,1,0:T(8,128)}, f32[8,32,128]{2,1,0:T(8,128)}) custom-call(f32[8,96,128]{2,1,0:T(8,128)} %get-tuple-element.127.refs_0_), custom_call_target="tpu_custom_call" | custom-call | tf_op jit(solution)/shard_map/pallas_call | solution.py:23
  95.0 0.0 collective-permute-done.8.refs_16_
  95.0 0.0 copy-start.2
  95.0 3.3 %collective-permute-start.9 = (f32[80,128]{1,0:T(8,128)S(1)}, f32[80,128]{1,0:T(8,128)S(1)}, u32[]{:S(2)}, u32[]{:S(2)}) collective-permute-start(f32[80,128]{1,0:T(8,128)S(1)} %add.33.refs_11_), channel_id=1, source_target_pairs={{0,128},{16,144},{32,160},{48,176},{64,192},{80,208},{96,224},{112... | collective-permute-start | bytes 122888 | tf_op jit(solution)/shard_map/ppermute | solution.py:206
  98.3 4.0 %shard_map.93 = (f32[8,32,128]{2,1,0:T(8,128)}, f32[8,32,128]{2,1,0:T(8,128)}, f32[8,32,128]{2,1,0:T(8,128)}) custom-call(f32[8,64,128]{2,1,0:T(8,128)} %get-tuple-element.135.refs_0_), custom_call_target="tpu_custom_call" | custom-call | tf_op jit(solution)/shard_map/pallas_call | solution.py:23
  102.3 0.0 collective-permute-done.9.refs_17_
  102.3 3.5 %collective-permute-start.10 = (f32[80,128]{1,0:T(8,128)S(1)}, f32[80,128]{1,0:T(8,128)S(1)}, u32[]{:S(2)}, u32[]{:S(2)}) collective-permute-start(f32[80,128]{1,0:T(8,128)S(1)} %add.34.refs_12_), channel_id=1, source_target_pairs={{0,384},{16,400},{32,416},{48,432},{64,448},{80,464},{96,480},{112... | collective-permute-start | bytes 122888 | tf_op jit(solution)/shard_map/ppermute | solution.py:206
  105.8 3.7 %shard_map.94 = (f32[8,32,128]{2,1,0:T(8,128)}, f32[8,32,128]{2,1,0:T(8,128)}) custom-call(f32[8,32,128]{2,1,0:T(8,128)} %get-tuple-element.143.refs_0_), custom_call_target="tpu_custom_call" | custom-call | tf_op jit(solution)/shard_map/pallas_call | solution.py:23
  109.5 0.0 collective-permute-done.10.refs_18_
  109.5 0.6 add.35.refs_13_
  110.2 0.0 copy-done.1
  110.2 13.7 %shard_map.95 = (f32[9,256,128]{2,1,0:T(8,128)}, f32[128,128]{1,0:T(8,128)}) custom-call(f32[128,128]{1,0:T(8,128)} %get-tuple-element.118.refs_0_, f32[8,32,128]{2,1,0:T(8,128)} %get-tuple-element.123.refs_1_, f32[8,32,128]{2,1,0:T(8,128)} %get-tuple-element.131.refs_2_, f32[8,32,128]{2,1,0:T(8,128)} %get-tuple-element.139.refs_3_, ...), custom_call_target="tpu_custom_call" | custom-call | tf_op jit(solution)/shard_map/pallas_call | solution.py:23
  (33 shorter events, 0.1 us)
Async XLA Ops:
  2.5 23.5 %collective-permute-start = (f32[576,128]{1,0:T(8,128)}, f32[576,128]{1,0:T(8,128)S(1)}, u32[]{:S(2)}, u32[]{:S(2)}) collective-permute-start(f32[576,128]{1,0:T(8,128)} %get-tuple-element.79), channel_id=1, source_target_pairs={{0,1},{1,2},{2,3},{3,4},{4,5},{5,6},{6,7},{7,8},{8,9},{9,10},{10,1... | collective-permute-start | bytes 884744 | tf_op jit(solution)/shard_map/ppermute | solution.py:202
  6.9 19.2 %collective-permute-start.1 = (f32[576,128]{1,0:T(8,128)}, f32[576,128]{1,0:T(8,128)S(1)}, u32[]{:S(2)}, u32[]{:S(2)}) collective-permute-start(f32[576,128]{1,0:T(8,128)} %get-tuple-element.80), channel_id=1, source_target_pairs={{1,0},{2,1},{3,2},{4,3},{5,4},{6,5},{7,6},{8,7},{9,8},{10,9},{11,1... | collective-permute-start | bytes 884744 | tf_op jit(solution)/shard_map/ppermute | solution.py:202
  26.1 0.7 copy-start.8
  26.1 0.8 copy-start.9
  34.1 6.4 %collective-permute-start.2 = (f32[80,128]{1,0:T(8,128)}, f32[80,128]{1,0:T(8,128)S(1)}, u32[]{:S(2)}, u32[]{:S(2)}) collective-permute-start(f32[80,128]{1,0:T(8,128)} %get-tuple-element.86), channel_id=1, source_target_pairs={{0,1},{1,0},{2,3},{3,2},{4,5},{5,4},{6,7},{7,6},{8,9},{9,8},{10,11... | collective-permute-start | bytes 122888 | tf_op jit(solution)/shard_map/ppermute | solution.py:206
  40.5 34.6 %copy-start.15 = (f32[80,128]{1,0:T(8,128)}, f32[80,128]{1,0:T(8,128)S(1)}, u32[]{:S(2)}) copy-start(f32[80,128]{1,0:T(8,128)S(1)} %collective-permute-done.2.refs_4_) | copy-start | bytes 122884
  41.3 33.8 %copy-start.4 = (f32[80,128]{1,0:T(8,128)}, f32[80,128]{1,0:T(8,128)S(1)}, u32[]{:S(2)}) copy-start(f32[80,128]{1,0:T(8,128)S(1)} %add.27.refs_0_) | copy-start | bytes 122884
  41.3 7.8 %collective-permute-start.3 = (f32[80,128]{1,0:T(8,128)S(1)}, f32[80,128]{1,0:T(8,128)S(1)}, u32[]{:S(2)}, u32[]{:S(2)}) collective-permute-start(f32[80,128]{1,0:T(8,128)S(1)} %add.27.refs_0_), channel_id=1, source_target_pairs={{0,2},{1,3},{2,0},{3,1},{4,6},{5,7},{6,4},{7,5},{8,10},{9,11},{10,... | collective-permute-start | bytes 122888 | tf_op jit(solution)/shard_map/ppermute | solution.py:206
  49.1 26.0 %copy-start.16 = (f32[80,128]{1,0:T(8,128)}, f32[80,128]{1,0:T(8,128)S(1)}, u32[]{:S(2)}) copy-start(f32[80,128]{1,0:T(8,128)S(1)} %collective-permute-done.3.refs_5_) | copy-start | bytes 122884
  49.1 26.0 %copy-start.5 = (f32[80,128]{1,0:T(8,128)}, f32[80,128]{1,0:T(8,128)S(1)}, u32[]{:S(2)}) copy-start(f32[80,128]{1,0:T(8,128)S(1)} %add.28.refs_1_) | copy-start | bytes 122884
  49.2 13.8 %collective-permute-start.4 = (f32[80,128]{1,0:T(8,128)S(1)}, f32[80,128]{1,0:T(8,128)S(1)}, u32[]{:S(2)}, u32[]{:S(2)}) collective-permute-start(f32[80,128]{1,0:T(8,128)S(1)} %add.28.refs_1_), channel_id=1, source_target_pairs={{0,4},{1,5},{2,6},{3,7},{4,0},{5,1},{6,2},{7,3},{8,12},{9,13},{10,... | collective-permute-start | bytes 122888 | tf_op jit(solution)/shard_map/ppermute | solution.py:206
  63.0 12.2 %copy-start.17 = (f32[80,128]{1,0:T(8,128)}, f32[80,128]{1,0:T(8,128)S(1)}, u32[]{:S(2)}) copy-start(f32[80,128]{1,0:T(8,128)S(1)} %collective-permute-done.4.refs_6_) | copy-start | bytes 122884
  63.0 12.2 %copy-start.6 = (f32[80,128]{1,0:T(8,128)}, f32[80,128]{1,0:T(8,128)S(1)}, u32[]{:S(2)}) copy-start(f32[80,128]{1,0:T(8,128)S(1)} %add.29.refs_2_) | copy-start | bytes 122884
  63.0 12.2 %collective-permute-start.5 = (f32[80,128]{1,0:T(8,128)S(1)}, f32[80,128]{1,0:T(8,128)S(1)}, u32[]{:S(2)}, u32[]{:S(2)}) collective-permute-start(f32[80,128]{1,0:T(8,128)S(1)} %add.29.refs_2_), channel_id=1, source_target_pairs={{0,15},{1,14},{2,13},{3,12},{4,11},{5,10},{6,9},{7,8},{8,7},{9,6},... | collective-permute-start | bytes 122888 | tf_op jit(solution)/shard_map/ppermute | solution.py:206
  75.2 8.6 %copy-start.18 = (f32[80,128]{1,0:T(8,128)}, f32[80,128]{1,0:T(8,128)S(1)}, u32[]{:S(2)}) copy-start(f32[80,128]{1,0:T(8,128)S(1)} %collective-permute-done.5.refs_7_) | copy-start | bytes 122884
  75.2 8.6 %copy-start.7 = (f32[80,128]{1,0:T(8,128)}, f32[80,128]{1,0:T(8,128)S(1)}, u32[]{:S(2)}) copy-start(f32[80,128]{1,0:T(8,128)S(1)} %add.30.refs_3_) | copy-start | bytes 122884
  75.2 6.6 %collective-permute-start.6 = (f32[80,128]{1,0:T(8,128)S(1)}, f32[80,128]{1,0:T(8,128)S(1)}, u32[]{:S(2)}, u32[]{:S(2)}) collective-permute-start(f32[80,128]{1,0:T(8,128)S(1)} %add.30.refs_3_), channel_id=1, source_target_pairs={{0,16},{16,0},{32,48},{48,32},{64,80},{80,64},{96,112},{112,96},{1... | collective-permute-start | bytes 122888 | tf_op jit(solution)/shard_map/ppermute | solution.py:206
  81.8 28.3 %copy-start.10 = (f32[80,128]{1,0:T(8,128)}, f32[80,128]{1,0:T(8,128)S(1)}, u32[]{:S(2)}) copy-start(f32[80,128]{1,0:T(8,128)S(1)} %collective-permute-done.6.refs_14_) | copy-start | bytes 122884
  81.8 28.3 %copy-start = (f32[80,128]{1,0:T(8,128)}, f32[80,128]{1,0:T(8,128)S(1)}, u32[]{:S(2)}) copy-start(f32[80,128]{1,0:T(8,128)S(1)} %add.31.refs_9_) | copy-start | bytes 122884
  81.8 6.1 %collective-permute-start.7 = (f32[80,128]{1,0:T(8,128)S(1)}, f32[80,128]{1,0:T(8,128)S(1)}, u32[]{:S(2)}, u32[]{:S(2)}) collective-permute-start(f32[80,128]{1,0:T(8,128)S(1)} %add.31.refs_9_), channel_id=1, source_target_pairs={{0,32},{16,48},{32,0},{48,16},{64,96},{80,112},{96,64},{112,80},{1... | collective-permute-start | bytes 122888 | tf_op jit(solution)/shard_map/ppermute | solution.py:206
  88.0 22.2 %copy-start.11 = (f32[80,128]{1,0:T(8,128)}, f32[80,128]{1,0:T(8,128)S(1)}, u32[]{:S(2)}) copy-start(f32[80,128]{1,0:T(8,128)S(1)} %collective-permute-done.7.refs_15_) | copy-start | bytes 122884
  88.0 22.2 %copy-start.1 = (f32[80,128]{1,0:T(8,128)}, f32[80,128]{1,0:T(8,128)S(1)}, u32[]{:S(2)}) copy-start(f32[80,128]{1,0:T(8,128)S(1)} %add.32.refs_10_) | copy-start | bytes 122884
  88.0 7.0 %collective-permute-start.8 = (f32[80,128]{1,0:T(8,128)S(1)}, f32[80,128]{1,0:T(8,128)S(1)}, u32[]{:S(2)}, u32[]{:S(2)}) collective-permute-start(f32[80,128]{1,0:T(8,128)S(1)} %add.32.refs_10_), channel_id=1, source_target_pairs={{0,96},{16,112},{32,64},{48,80},{64,32},{80,48},{96,0},{112,16},{1... | collective-permute-start | bytes 122888 | tf_op jit(solution)/shard_map/ppermute | solution.py:206
  95.0 15.1 %copy-start.12 = (f32[80,128]{1,0:T(8,128)}, f32[80,128]{1,0:T(8,128)S(1)}, u32[]{:S(2)}) copy-start(f32[80,128]{1,0:T(8,128)S(1)} %collective-permute-done.8.refs_16_) | copy-start | bytes 122884
  95.0 15.1 %copy-start.2 = (f32[80,128]{1,0:T(8,128)}, f32[80,128]{1,0:T(8,128)S(1)}, u32[]{:S(2)}) copy-start(f32[80,128]{1,0:T(8,128)S(1)} %add.33.refs_11_) | copy-start | bytes 122884
  95.0 7.3 %collective-permute-start.9 = (f32[80,128]{1,0:T(8,128)S(1)}, f32[80,128]{1,0:T(8,128)S(1)}, u32[]{:S(2)}, u32[]{:S(2)}) collective-permute-start(f32[80,128]{1,0:T(8,128)S(1)} %add.33.refs_11_), channel_id=1, source_target_pairs={{0,128},{16,144},{32,160},{48,176},{64,192},{80,208},{96,224},{112... | collective-permute-start | bytes 122888 | tf_op jit(solution)/shard_map/ppermute | solution.py:206
  102.3 7.9 %copy-start.13 = (f32[80,128]{1,0:T(8,128)}, f32[80,128]{1,0:T(8,128)S(1)}, u32[]{:S(2)}) copy-start(f32[80,128]{1,0:T(8,128)S(1)} %collective-permute-done.9.refs_17_) | copy-start | bytes 122884
  102.3 7.9 %copy-start.3 = (f32[80,128]{1,0:T(8,128)}, f32[80,128]{1,0:T(8,128)S(1)}, u32[]{:S(2)}) copy-start(f32[80,128]{1,0:T(8,128)S(1)} %add.34.refs_12_) | copy-start | bytes 122884
  102.3 7.2 %collective-permute-start.10 = (f32[80,128]{1,0:T(8,128)S(1)}, f32[80,128]{1,0:T(8,128)S(1)}, u32[]{:S(2)}, u32[]{:S(2)}) collective-permute-start(f32[80,128]{1,0:T(8,128)S(1)} %add.34.refs_12_), channel_id=1, source_target_pairs={{0,384},{16,400},{32,416},{48,432},{64,448},{80,464},{96,480},{112... | collective-permute-start | bytes 122888 | tf_op jit(solution)/shard_map/ppermute | solution.py:206
  109.5 0.7 copy-start.14
